TPU v7x, 512 devices: a whole 4x4x16 slice. The times are simulated.
512 devices in a mesh: expert: 16 (over x, y), tensor: 32 (over z, core).
Axes of the slice: x: 4, y: 4, z: 16, core: 2. Of those that a mesh axis runs over, the one named last changes fastest.
Arguments:
- tokens: bfloat16 [1024, 4096], P('expert', 'tensor'), may hold values from -6 to 6
- routes: int32 [1024, 2], P('expert'), may hold values from 0 to 7, all different within a row; in each aligned block of 64 rows (0 to 63, 64 to 127, ...) at most 32 rows name the same one
- route_weight: float32 [1024, 2], P('expert'), may hold values from 0.25 to 1
- gate_weight: bfloat16 [16, 5504, 4096], P('expert', 'tensor'), may hold values from -0.09375 to 0.09375
- up_weight: bfloat16 [16, 5504, 4096], P('expert', 'tensor'), may hold values from -0.09375 to 0.09375
- down_weight: bfloat16 [16, 5504, 4096], P('expert', 'tensor'), may hold values from -0.109375 to 0.109375
Outputs:
- mixed: bfloat16 [1024, 4096], P('expert', 'tensor')
Inputs may be any that keep to these rules, and one draw needn't show every extreme that they name: `routes`: each row names two different experts; within the 64 rows of one index of expert no expert is named more than 32 times, a bound that some block reaches.
All inputs are finite; a program needn't handle non-finite values.
Results may differ from a plain program's by a relative error of at most 0.024.
Values may be sent and summed in bfloat16 or wider, within the bound.
No kernel may reach another device: no remote copies, remote signals or barrier semaphores. Data moves between devices by JAX's collectives and lax.ppermute only.
A program may use at most 64 MiB of HBM per device.

v0:
```python
import jax
import jax.numpy as jnp
from jax import lax
from jax.sharding import Mesh
from jax.sharding import PartitionSpec as P

TENSOR = ("tensor_0", "tensor_1")


def own_block(parts, axes, sequence):
    lengths = [lax.axis_size(a) for a in axes]
    parts = parts.reshape(*lengths, *parts.shape[1:])
    parts = parts.transpose(*sequence, *range(len(axes), parts.ndim))
    parts = parts.reshape(-1, *parts.shape[len(axes) :])
    for k in sequence:
        parts = lax.psum_scatter(parts, axes[k], scatter_dimension=0, tiled=True)
    return parts[0]


def cut_along(x, dim, count):
    lengths = x.shape
    parts = x.reshape(*lengths[:dim], count, lengths[dim] // count, *lengths[dim + 1 :])
    return jnp.moveaxis(parts, dim, 0)


def summed_rows(x, axes, sequence, dim):
    count = lax.axis_size(axes)
    return own_block(cut_along(x, dim, count), axes, sequence)


def slot_positions(route_block, experts, capacity):
    flat_routes = route_block.reshape(-1)
    onehot = (flat_routes[:, None] == jnp.arange(experts, dtype=jnp.int32)[None, :]).astype(
        jnp.int32
    )
    earlier = jnp.cumsum(onehot, axis=0) - onehot
    slot_index = jnp.sum(earlier * onehot, axis=1)
    return (flat_routes * capacity + slot_index).reshape(route_block.shape)


def feature_product(rows, weight_rows):
    return lax.dot_general(
        rows, weight_rows, (((1,), (1,)), ((), ())), preferred_element_type=jnp.float32
    )


def local(tokens, routes, route_weight, gate_weight, up_weight, down_weight):
    group_count = lax.axis_size("expert")
    experts = group_count // 2
    tok_rows = routes.shape[0]
    capacity = min(tok_rows, 4 * tok_rows // experts)
    slots_out = experts * capacity
    slots_in = group_count * capacity
    positions = slot_positions(routes, experts, capacity)
    slot_ids = jnp.arange(slots_out, dtype=jnp.int32)
    matches = positions[:, :, None] == slot_ids[None, None, :]
    select = jnp.any(matches, axis=1).astype(jnp.bfloat16).T
    combine_matrix = jnp.sum(jnp.where(matches, route_weight[:, :, None], 0.0), axis=1)
    w_gate = gate_weight[0]
    w_up = up_weight[0]
    w_down = down_weight[0]
    outgoing = jnp.dot(select, tokens, preferred_element_type=jnp.float32).astype(jnp.bfloat16)
    outgoing = outgoing.reshape(experts, capacity, tokens.shape[1])
    outgoing = jnp.repeat(outgoing, 2, axis=0)
    incoming = lax.all_to_all(outgoing, "expert", split_axis=0, concat_axis=0, tiled=True)
    incoming = incoming.reshape(slots_in, tokens.shape[1])
    segment = lax.all_gather(incoming, TENSOR, axis=1, tiled=True)
    gate_sum = feature_product(segment, w_gate)
    up_sum = feature_product(segment, w_up)
    hidden = (jax.nn.silu(gate_sum) * up_sum).astype(jnp.bfloat16)
    partial_value = jnp.dot(hidden, w_down, preferred_element_type=jnp.float32)
    summed = (
        summed_rows(partial_value.astype(jnp.bfloat16), TENSOR, (1, 0), 1)
        .astype(jnp.float32)
        .astype(jnp.bfloat16)
    )
    summed = summed.reshape(group_count, capacity, summed.shape[1])
    returned = lax.all_to_all(summed, "expert", split_axis=0, concat_axis=0, tiled=True)
    returned = returned.reshape(experts, 2, capacity, returned.shape[2]).astype(jnp.float32)
    returned = jnp.sum(returned, axis=1).reshape(slots_out, returned.shape[3])
    mixed = jnp.dot(combine_matrix, returned, preferred_element_type=jnp.float32)
    return mixed.astype(jnp.bfloat16)


def solution(mesh):
    torus = Mesh(
        mesh.devices.reshape(mesh.shape["expert"], 16, 2), ("expert", "tensor_0", "tensor_1")
    )
    placed = (
        P("expert", TENSOR),
        P("expert", None),
        P("expert", None),
        P("expert", TENSOR, None),
        P("expert", TENSOR, None),
        P("expert", TENSOR, None),
    )
    return jax.shard_map(
        local, mesh=torus, in_specs=placed, out_specs=P("expert", TENSOR), check_vma=False
    )
```

profile of v0, /device:TPU:2, one launch (start us, length us, event | category | flops | bytes accessed | tf_op | source)
XLA Modules:
  0.0 241.0 jit_solution(17170054576650611929)
XLA Ops:
  6.5 0.0 copy-start
  6.5 0.9 copy.27
  7.4 0.1 eq.28
  7.6 0.1 fusion.21
  7.7 0.2 reduce_window_sum.11
  7.8 0.2 select_reduce_fusion.1
  8.0 0.1 reduce_sum.30
  8.2 0.1 copy.28
  8.2 0.7 multiply_add_fusion
  8.9 0.1 fusion.20
  9.0 0.9 convolution_convert_fusion.1
  10.0 15.4 %all_to_all.10 = bf16[16,32,128]{2,1,0:T(8,128)(2,1)} all-to-all(bf16[16,32,128]{2,1,0:T(8,128)(2,1)S(1)} %bitcast.43), channel_id=1, replica_groups=mesh['expert'=16,'tensor_0'=16,'tensor_1'=2] {'expert'}, dimensions={0} | all-to-all | bytes 262144 | tf_op jit(solution)/shard_map/all_to_all | solution.py:65
  25.4 0.0 all-gather.2.cloned.1.call-update
  25.4 0.0 copy-start.1
  25.5 0.0 reduce-scatter.3.cloned.1.call-start
  25.5 81.2 %all-gather.2.cloned.1.call-done = bf16[512,4096]{1,0:T(8,128)(2,1)} async-done(((bf16[512,128]{1,0:T(8,128)(2,1)}), bf16[512,4096]{1,0:T(8,128)(2,1)}) %all-gather.2.cloned.1.call-update) | async-done | bytes 4194320 | tf_op jit(solution)/shard_map/all_gather | solution.py:67
  106.7 4.2 %fusion.4 = f32[512,172]{0,1:T(8,128)S(1)} fusion(bf16[512,4096]{1,0:T(8,128)(2,1)} %all-gather.2.cloned.1.call-done, bf16[1,172,4096]{2,1,0:T(8,128)(2,1)} %param.9), kind=kOutput, calls=%fused_computation.6 | convolution fusion | flops 721420288 | bytes 5955584 | tf_op jit(solution)/shard_map/dot_general | solution.py:42
  110.9 0.0 copy-done
  110.9 0.0 copy-done.1
  110.9 7.0 %fusion = bf16[64,32,8,128]{3,2,1,0:T(8,128)(2,1)} fusion(bf16[1,172,4096]{2,1,0:T(8,128)(2,1)S(1)} %copy-done, bf16[512,4096]{1,0:T(8,128)(2,1)} %all-gather.2.cloned.1.call-done, bf16[1,172,4096]{2,1,0:T(8,128)(2,1)S(1)} %copy-done.1, f32[512,172]{0,1:T(8,128)S(1)} %fusion.4), kind=kOutput, calls=%fused_computation.2 | convolution fusion | flops 1445466112 | bytes 11558912 | tf_op jit(solution)/shard_map/dot_general | solution.py:71
  117.9 3.3 %copy.33 = bf16[64,32,8,128]{3,2,0,1:T(8,128)(2,1)S(1)} copy(bf16[64,32,8,128]{3,2,1,0:T(8,128)(2,1)} %fusion) | data formatting | bytes 8388608 | tf_op jit(solution)/shard_map/reshape | solution.py:22
  121.3 2.2 copy.30
  123.5 0.0 reduce-scatter.3.cloned.1.call-update
  123.5 0.0 copy-start.2
  123.5 0.0 reduce-scatter.5.cloned.1.call-start
  123.6 18.1 %reduce-scatter.3.cloned.1.call-done = bf16[16,512,128]{2,1,0:T(8,128)(2,1)} async-done(((bf16[32,512,128]{2,1,0:T(8,128)(2,1)}), bf16[16,512,128]{2,1,0:T(8,128)(2,1)}) %reduce-scatter.3.cloned.1.call-update) | async-done | bytes 2097168 | tf_op jit(solution)/shard_map/reduce_scatter | solution.py:16
  141.7 0.0 reduce-scatter.5.cloned.1.call-update
  141.7 78.2 %reduce-scatter.5.cloned.1.call-done = bf16[1,512,128]{2,1,0:T(8,128)(2,1)} async-done(((bf16[16,512,128]{2,1,0:T(8,128)(2,1)}), bf16[1,512,128]{2,1,0:T(8,128)(2,1)}) %reduce-scatter.5.cloned.1.call-update) | async-done | bytes 131088 | tf_op jit(solution)/shard_map/reduce_scatter | solution.py:16
  219.9 7.4 %all-to-all-start.1 = ((bf16[16,32,128]{2,1,0:T(8,128)(2,1)}), bf16[16,32,128]{2,1,0:T(8,128)(2,1)S(1)}, u32[]{:S(2)}, u32[]{:S(2)}) async-start(bf16[16,32,128]{2,1,0:T(8,128)(2,1)} %bitcast.46), calls=%async_computation.3 | async-start | bytes 262144 | tf_op jit(solution)/shard_map/all_to_all | solution.py:78
  227.3 0.1 select_reduce_fusion
  227.4 6.3 %all-to-all-done.1 = bf16[16,32,128]{2,1,0:T(8,128)(2,1)S(1)} async-done(((bf16[16,32,128]{2,1,0:T(8,128)(2,1)}), bf16[16,32,128]{2,1,0:T(8,128)(2,1)S(1)}, u32[]{:S(2)}, u32[]{:S(2)}) %all-to-all-start.1) | async-done | bytes 131104 | tf_op jit(solution)/shard_map/all_to_all | solution.py:78
  233.7 0.7 fusion.23
  (4 shorter events, 0.0 us)
Async XLA Ops:
  6.5 104.3 %copy-start = (bf16[1,172,4096]{2,1,0:T(8,128)(2,1)S(1)}, bf16[1,172,4096]{2,1,0:T(8,128)(2,1)}, u32[]{:S(2)}) copy-start(bf16[1,172,4096]{2,1,0:T(8,128)(2,1)} %param.11) | copy-start | bytes 4227076
  6.5 100.2 %all-gather.2.cloned.1.call-start = ((), (), s32[]{:S(2)}) async-start(), calls=%async_computation.4 | async-start | bytes 4325376 | tf_op jit(solution)/shard_map/all_gather | solution.py:67
  25.4 85.4 %copy-start.1 = (bf16[1,172,4096]{2,1,0:T(8,128)(2,1)S(1)}, bf16[1,172,4096]{2,1,0:T(8,128)(2,1)}, u32[]{:S(2)}) copy-start(bf16[1,172,4096]{2,1,0:T(8,128)(2,1)} %param.10) | copy-start | bytes 4227076
  25.5 116.2 %reduce-scatter.3.cloned.1.call-start = ((), (), s32[]{:S(2)}) async-start(), calls=%async_computation.5 | async-start | bytes 6291456 | tf_op jit(solution)/shard_map/reduce_scatter | solution.py:16
  123.5 103.8 %copy-start.2 = (f32[64,2]{0,1:T(2,128)S(1)}, f32[64,2]{0,1:T(2,128)}, u32[]{:S(2)}) copy-start(f32[64,2]{0,1:T(2,128)} %param.8) | copy-start | bytes 1540
  123.5 96.4 %reduce-scatter.5.cloned.1.call-start = ((), (), s32[]{:S(2)}) async-start(), calls=%async_computation.6 | async-start | bytes 2228224 | tf_op jit(solution)/shard_map/reduce_scatter | solution.py:16
  219.9 13.8 %all-to-all-start.1 = ((bf16[16,32,128]{2,1,0:T(8,128)(2,1)}), bf16[16,32,128]{2,1,0:T(8,128)(2,1)S(1)}, u32[]{:S(2)}, u32[]{:S(2)}) async-start(bf16[16,32,128]{2,1,0:T(8,128)(2,1)} %bitcast.46), calls=%async_computation.3 | async-start | bytes 262144 | tf_op jit(solution)/shard_map/all_to_all | solution.py:78
Sparse Core Ops, SparseCore 0:
  25.6 81.0 all-gather.1
  123.6 17.9 reduce-scatter.2
  144.5 75.3 reduce-scatter.4
where the time goes:
time: 241 us
  waiting for transfers between devices  184 us (76%)
  blocking collectives  15.4 us (6%)
  between operations  13.2 us (5%)
  matrix products  12.9 us (5%)
  starting transfers between devices  7.53 us (3%)
  local copies, waits for them, and re-layouts  6.83 us (3%)
    reduce_scatter x2, waiting for transfers between devices, own_block(): parts = lax.psum_scatter(parts, axes[k], scatter_dimension=0, tiled=True)  96.3 us
    all_gather x1, waiting for transfers between devices, local(): segment = lax.all_gather(incoming, TENSOR, axis=1, tiled=True)  81.2 us
    all_to_all x1, blocking collectives, local(): lax.all_to_all(outgoing, 'expert', split_axis=0, concat_axis=0, tiled=True)  15.4 us
    all_to_all x1, starting transfers between devices, local(): lax.all_to_all(summed, 'expert', split_axis=0, concat_axis=0, tiled=True)  7.44 us
    dot_general x1, matrix products, local(): partial_value = jnp.dot(hidden, w_down, preferred_element_type=jnp.float32)  7.03 us
    all_to_all x1, waiting for transfers between devices, local(): lax.all_to_all(summed, 'expert', split_axis=0, concat_axis=0, tiled=True)  6.28 us
  transfers between devices with their start and end apart: 4, of which 4 were waited for; matrix products, arithmetic and copies ran while one was open for 0% of the time, Pallas kernels for 0%

commit v1 on v0

v1 whole, which is shorter than its diff:
```python
import jax
import jax.numpy as jnp
from jax import lax
from jax.experimental import pallas as pl
from jax.experimental.pallas import tpu as pltpu
from jax.sharding import Mesh
from jax.sharding import PartitionSpec as P

BF = jnp.bfloat16
F32 = jnp.float32
TENSOR = ("tensor_0", "tensor_1")


def split_weights(core, gate, up, down):
    units, width = gate.shape
    half = width // 2
    step = 512

    def kernel(core_ref, g_ref, u_ref, d_ref, kg_ref, ku_ref, kd_ref, send_ref):
        c = core_ref[0]
        for i, (src, keep) in enumerate(((g_ref, kg_ref), (u_ref, ku_ref), (d_ref, kd_ref))):
            for j in range(step // 128):
                mine = pl.multiple_of((2 * j + c) * 128, 128)
                other = pl.multiple_of((2 * j + 1 - c) * 128, 128)
                keep[:, j * 128 : (j + 1) * 128] = src[:, pl.ds(mine, 128)]
                send_ref[i, :, j * 128 : (j + 1) * 128] = src[:, pl.ds(other, 128)]

    src_spec = pl.BlockSpec((units, 2 * step), lambda i, c: (0, i))
    keep_spec = pl.BlockSpec((units, step), lambda i, c: (0, i))
    return pl.pallas_call(
        kernel,
        grid_spec=pltpu.PrefetchScalarGridSpec(
            num_scalar_prefetch=1,
            grid=(half // step,),
            in_specs=[src_spec] * 3,
            out_specs=[keep_spec] * 3 + [pl.BlockSpec((3, units, step), lambda i, c: (0, 0, i))],
        ),
        out_shape=[jax.ShapeDtypeStruct((units, half), BF)] * 3
        + [jax.ShapeDtypeStruct((3, units, half), BF)],
        name="split_weights",
        cost_estimate=pl.CostEstimate(flops=0, bytes_accessed=12 * units * width, transcendentals=0),
    )(core, gate, up, down)


def dispatch(select, gathered, experts, capacity):
    planes, rows, lanes = gathered.shape
    per = 4

    def kernel(s_ref, x_ref, o_ref):
        x = jnp.concatenate([x_ref[k] for k in range(per)], axis=1)
        y = jnp.dot(s_ref[...], x, preferred_element_type=F32).astype(BF)
        y = y.reshape(experts, capacity, per * lanes)
        o_ref[:, 0] = y
        o_ref[:, 1] = y

    return pl.pallas_call(
        kernel,
        grid=(planes // per,),
        in_specs=[
            pl.BlockSpec(select.shape, lambda i: (0, 0)),
            pl.BlockSpec((per, rows, lanes), lambda i: (i, 0, 0)),
        ],
        out_specs=pl.BlockSpec((experts, 2, capacity, per * lanes), lambda i: (0, 0, 0, i)),
        out_shape=jax.ShapeDtypeStruct((experts, 2, capacity, planes * lanes), BF),
        name="dispatch",
    )(select, gathered)


def padded(units):
    return -(-units // 8) * 8


def dot_last(a, b):
    return lax.dot_general(a, b, (((1,), (1,)), ((), ())), preferred_element_type=F32)


def gate_up(rows_in, keep_gate, keep_up, other):
    count, half = rows_in.shape
    units = keep_gate.shape[0]
    tall = padded(units)
    step = 512

    def kernel(x_ref, g_ref, u_ref, og_ref, ou_ref, o_ref):
        x = x_ref[...]
        parts = (g_ref[...], og_ref[0], u_ref[...], ou_ref[0])
        first = pl.program_id(0) == 0
        for i, w in enumerate(parts):
            total = dot_last(w, x)

            @pl.when(first)
            def _():
                o_ref[i * tall : i * tall + units] = total

            @pl.when(jnp.logical_not(first))
            def _():
                o_ref[i * tall : i * tall + units] += total

    return pl.pallas_call(
        kernel,
        grid=(half // step,),
        in_specs=[
            pl.BlockSpec((count, step), lambda i: (0, i)),
            pl.BlockSpec((units, step), lambda i: (0, i)),
            pl.BlockSpec((units, step), lambda i: (0, i)),
            pl.BlockSpec((1, units, step), lambda i: (0, 0, i)),
            pl.BlockSpec((1, units, step), lambda i: (1, 0, i)),
        ],
        out_specs=pl.BlockSpec((4 * tall, count), lambda i: (0, 0)),
        out_shape=jax.ShapeDtypeStruct((4 * tall, count), F32),
        name="gate_up",
    )(rows_in, keep_gate, keep_up, other, other)


def down_rows(own, received, keep_down, other):
    count = own.shape[1]
    units, half = keep_down.shape
    tall = padded(units)
    step = 512

    def part(ref, k):
        return ref[k * tall : k * tall + units]

    def kernel(p_ref, r_ref, d_ref, od_ref, o_ref, mine, partner):
        @pl.when(pl.program_id(0) == 0)
        def _():
            for k, out in ((0, mine), (1, partner)):
                gate = part(p_ref, k) + part(r_ref, 1 - k)
                up = part(p_ref, 2 + k) + part(r_ref, 3 - k)
                hidden = gate / (1.0 + jnp.exp(-gate)) * up
                out[...] = hidden.T.astype(BF)

        total = jnp.dot(mine[...], d_ref[...], preferred_element_type=F32)
        total += jnp.dot(partner[...], od_ref[0], preferred_element_type=F32)
        o_ref[...] = total.astype(BF)

    whole = pl.BlockSpec((4 * tall, count), lambda i: (0, 0))
    return pl.pallas_call(
        kernel,
        grid=(half // step,),
        in_specs=[
            whole,
            whole,
            pl.BlockSpec((units, step), lambda i: (0, i)),
            pl.BlockSpec((1, units, step), lambda i: (2, 0, i)),
        ],
        out_specs=pl.BlockSpec((count, step), lambda i: (0, i)),
        out_shape=jax.ShapeDtypeStruct((count, half), BF),
        scratch_shapes=[pltpu.VMEM((count, units), BF)] * 2,
        name="down_rows",
    )(own, received, keep_down, other)


def combine(weights, returned, planes):
    twice, slots = weights.shape
    rows = twice // 2
    half = returned.shape[1]
    lanes = half // planes
    per = 4

    def kernel(w_ref, r_ref, o_ref):
        total = jnp.dot(w_ref[...], r_ref[...], preferred_element_type=F32)
        total = (total[:rows] + total[rows:]).astype(BF)
        for k in range(per):
            o_ref[k] = total[:, k * lanes : (k + 1) * lanes]

    return pl.pallas_call(
        kernel,
        grid=(planes // per,),
        in_specs=[
            pl.BlockSpec((twice, slots), lambda i: (0, 0)),
            pl.BlockSpec((slots, per * lanes), lambda i: (0, i)),
        ],
        out_specs=pl.BlockSpec((per, rows, lanes), lambda i: (i, 0, 0)),
        out_shape=jax.ShapeDtypeStruct((planes, rows, lanes), BF),
        name="combine",
    )(weights, returned)


def slot_positions(route_block, experts, capacity):
    flat_routes = route_block.reshape(-1)
    onehot = (flat_routes[:, None] == jnp.arange(experts, dtype=jnp.int32)[None, :]).astype(
        jnp.int32
    )
    earlier = jnp.cumsum(onehot, axis=0) - onehot
    slot_index = jnp.sum(earlier * onehot, axis=1)
    return (flat_routes * capacity + slot_index).reshape(route_block.shape)


def local(tokens, routes, route_weight, gate_weight, up_weight, down_weight):
    group_count = lax.axis_size("expert")
    planes = lax.axis_size("tensor_0")
    experts = group_count // 2
    tok_rows, lanes = tokens.shape
    capacity = min(tok_rows, 4 * tok_rows // experts)
    slots_out = experts * capacity
    slots_in = group_count * capacity
    half = planes * lanes
    core = lax.axis_index("tensor_1").astype(jnp.int32).reshape(1)

    spread = jnp.broadcast_to(tokens[None], (planes, tok_rows, lanes))
    gathered = lax.all_to_all(spread, "tensor_0", split_axis=0, concat_axis=0, tiled=True)

    positions = slot_positions(routes, experts, capacity)
    slot_ids = jnp.arange(slots_out, dtype=jnp.int32)
    matches = positions[:, :, None] == slot_ids[None, None, :]
    select = jnp.any(matches, axis=1).astype(BF).T
    mix = jnp.sum(jnp.where(matches, route_weight[:, :, None], 0.0), axis=1)
    mix = mix.reshape(tok_rows, experts, 1, capacity)
    mix = jnp.broadcast_to(mix, (tok_rows, experts, 2, capacity)).reshape(tok_rows, slots_in)
    high = lax.reduce_precision(mix, 8, 7)
    mix = jnp.concatenate([high, mix - high], axis=0).astype(BF)

    keep_gate, keep_up, keep_down, send = split_weights(
        core, gate_weight[0], up_weight[0], down_weight[0]
    )
    swap = [(0, 1), (1, 0)]
    other = lax.ppermute(send, "tensor_1", swap)

    outgoing = dispatch(select, gathered, experts, capacity)
    outgoing = outgoing.reshape(group_count, capacity, half)
    incoming = lax.all_to_all(outgoing, "expert", split_axis=0, concat_axis=0, tiled=True)
    incoming = incoming.reshape(slots_in, half)

    own = gate_up(incoming, keep_gate, keep_up, other)
    received = lax.ppermute(own, "tensor_1", swap)
    result = down_rows(own, received, keep_down, other)

    result = result.reshape(group_count, capacity, half)
    returned = lax.all_to_all(result, "expert", split_axis=0, concat_axis=0, tiled=True)
    blocks = combine(mix, returned.reshape(slots_in, half), planes)
    blocks = lax.all_to_all(blocks, "tensor_0", split_axis=0, concat_axis=0, tiled=True)
    return jnp.sum(blocks.astype(F32), axis=0).astype(BF)


def solution(mesh):
    torus = Mesh(
        mesh.devices.reshape(mesh.shape["expert"], 16, 2), ("expert", "tensor_0", "tensor_1")
    )
    placed = (
        P("expert", TENSOR),
        P("expert", None),
        P("expert", None),
        P("expert", TENSOR, None),
        P("expert", TENSOR, None),
        P("expert", TENSOR, None),
    )
    return jax.shard_map(
        local, mesh=torus, in_specs=placed, out_specs=P("expert", TENSOR), check_vma=False
    )
```

time: 241 us -> 162 us (0.67)
  the two profiles are of different devices: /device:TPU:2 before, /device:TPU:32 now
where the time goes in v1:
time: 162 us; the launch traced here: 161 us
  waiting for transfers between devices  71.6 us (44%)
  starting transfers between devices  30.1 us (19%)
  Pallas kernels  27 us (17%)
  blocking collectives  24.4 us (15%)
  local copies, waits for them, and re-layouts  6.04 us (4%)
  other arithmetic  1.96 us (1%)
    all_to_all x1, waiting for transfers between devices, local(): lax.all_to_all(result, 'expert', split_axis=0, concat_axis=0, tiled=True)  30.2 us
    all_to_all x1, waiting for transfers between devices, local(): lax.all_to_all(outgoing, 'expert', split_axis=0, concat_axis=0, tiled=True)  29 us
    all_to_all x1, blocking collectives, local(): lax.all_to_all(blocks, 'tensor_0', split_axis=0, concat_axis=0, tiled=True)  24.4 us
    all_to_all x1, starting transfers between devices, local(): lax.all_to_all(spread, 'tensor_0', split_axis=0, concat_axis=0, tiled=True)  15.2 us
    all_to_all x1, waiting for transfers between devices, local(): lax.all_to_all(spread, 'tensor_0', split_axis=0, concat_axis=0, tiled=True)  8.98 us
    pallas_call x1, Pallas kernels, gate_up(): pl.pallas_call(kernel, grid=(half // step,), in_specs=[pl.BlockSpec((coun...  8.2 us
    all_to_all x1, starting transfers between devices, local(): lax.all_to_all(outgoing, 'expert', split_axis=0, concat_axis=0, tiled=True)  7.09 us
    pallas_call x1, Pallas kernels, down_rows(): pl.pallas_call(kernel, grid=(half // step,), in_specs=[whole, whole, pl.B...  5.95 us
  transfers between devices with their start and end apart: 5, of which 4 were waited for; matrix products, arithmetic and copies ran while one was open for 2% of the time, Pallas kernels for 6%

profile of v1, /device:TPU:32, one launch (start us, length us, event | category | flops | bytes accessed | tf_op | source)
XLA Modules:
  0.0 161.3 jit_solution(1582202707426535606)
XLA Ops:
  0.0 1.5 broadcast_in_dim.32
  1.5 15.2 %all-to-all-start = ((bf16[16,64,128]{2,1,0:T(8,128)(2,1)}), bf16[16,64,128]{2,1,0:T(8,128)(2,1)S(1)}, u32[]{:S(2)}, u32[]{:S(2)}) async-start(bf16[16,64,128]{2,1,0:T(8,128)(2,1)} %broadcast_in_dim.32), calls=%async_computation | async-start | bytes 524288 | tf_op jit(solution)/shard_map/all_to_all | solution.py:201
  16.7 5.2 %split_weights.1 = (bf16[172,2048]{1,0:T(8,128)(2,1)}, bf16[172,2048]{1,0:T(8,128)(2,1)}, bf16[172,2048]{1,0:T(8,128)(2,1)}, bf16[3,172,2048]{2,1,0:T(8,128)(2,1)}) custom-call(s32[1]{0:T(128)} %bitcast.5.core_ref, bf16[172,4096]{1,0:T(8,128)(2,1)} %bitcast.14, bf16[172,4096]{1,0:T(8,128)(2,1)} %bitcast.15, bf16[172,4096]{1,0:T(8,128)(2,1)} %bitcast.16), custom_call_target="tpu_custom_call" | custom-call | bytes 8454144 | tf_op jit(solution)/shard_map/split_weights/pallas_call | solution.py:30
  21.9 1.9 %collective-permute-start = (bf16[3,172,2048]{2,1,0:T(8,128)(2,1)}, bf16[3,172,2048]{2,1,0:T(8,128)(2,1)S(1)}, u32[]{:S(2)}, u32[]{:S(2)}) collective-permute-start(bf16[3,172,2048]{2,1,0:T(8,128)(2,1)} %get-tuple-element.11), channel_id=1, source_target_pairs={{0,1},{1,0},{2,3},{3,2},{4,5},{5,4},{6,7},{7,6},{8,9},{9,8},{10,11... | collective-permute-start | bytes 6340616 | tf_op jit(solution)/shard_map/ppermute | solution.py:217
  23.9 0.1 copy.25
  24.0 0.1 eq.28
  24.1 0.1 fusion.2
  24.2 0.2 reduce_window_sum.11
  24.4 0.2 select_reduce_fusion.1
  24.5 0.1 reduce_sum.33
  24.8 0.1 fusion.1
  24.9 0.7 copy.30
  25.6 9.0 %all-to-all-done.x_ref = bf16[16,64,128]{2,1,0:T(8,128)(2,1)S(1)} async-done(((bf16[16,64,128]{2,1,0:T(8,128)(2,1)}), bf16[16,64,128]{2,1,0:T(8,128)(2,1)S(1)}, u32[]{:S(2)}, u32[]{:S(2)}) %all-to-all-start) | async-done | bytes 262176 | tf_op jit(solution)/shard_map/all_to_all | solution.py:201
  34.6 0.7 copy-done.3
  35.3 3.8 %dispatch.1 = bf16[8,2,32,2048]{3,2,1,0:T(8,128)(2,1)} custom-call(bf16[256,64]{1,0:T(8,128)(2,1)} %bitcast.19, bf16[16,64,128]{2,1,0:T(8,128)(2,1)} %copy-done.3), custom_call_target="tpu_custom_call" | custom-call | tf_op jit(solution)/shard_map/dispatch/pallas_call | solution.py:56
  39.1 7.1 %all-to-all-start.1 = ((bf16[16,32,2048]{2,1,0:T(8,128)(2,1)}), bf16[16,32,2048]{2,1,0:T(8,128)(2,1)}, u32[]{:S(2)}, u32[]{:S(2)}) async-start(bf16[16,32,2048]{2,1,0:T(8,128)(2,1)} %bitcast.12), calls=%async_computation.1 | async-start | bytes 4194304 | tf_op jit(solution)/shard_map/all_to_all | solution.py:221
  46.2 29.0 %all-to-all-done.1 = bf16[16,32,2048]{2,1,0:T(8,128)(2,1)} async-done(((bf16[16,32,2048]{2,1,0:T(8,128)(2,1)}), bf16[16,32,2048]{2,1,0:T(8,128)(2,1)}, u32[]{:S(2)}, u32[]{:S(2)}) %all-to-all-start.1) | async-done | bytes 2097184 | tf_op jit(solution)/shard_map/all_to_all | solution.py:221
  75.2 8.2 %gate_up.1.p_ref = f32[704,512]{1,0:T(8,128)} custom-call(bf16[512,2048]{1,0:T(8,128)(2,1)} %bitcast.4.x_ref, bf16[172,2048]{1,0:T(8,128)(2,1)} %get-tuple-element.9.g_ref, bf16[172,2048]{1,0:T(8,128)(2,1)} %get-tuple-element.10.u_ref, bf16[3,172,2048]{2,1,0:T(8,128)(2,1)} %copy-done, bf16[3,172,2048]{2,1,0:T(8,128)(2,1)} %copy-done), custom_call_target="tpu_custom_call" | custom-call | tf_op jit(solution)/shard_map/gate_up/pallas_call | solution.py:98
  83.4 1.9 %collective-permute-start.1 = (f32[704,512]{1,0:T(8,128)}, f32[704,512]{1,0:T(8,128)S(1)}, u32[]{:S(2)}, u32[]{:S(2)}) collective-permute-start(f32[704,512]{1,0:T(8,128)} %gate_up.1.p_ref), channel_id=1, source_target_pairs={{0,1},{1,0},{2,3},{3,2},{4,5},{5,4},{6,7},{7,6},{8,9},{9,8},{10,11... | collective-permute-start | bytes 4325384 | tf_op jit(solution)/shard_map/ppermute | solution.py:225
  85.3 3.4 %collective-permute-done.1.r_ref = f32[704,512]{1,0:T(8,128)S(1)} collective-permute-done((f32[704,512]{1,0:T(8,128)}, f32[704,512]{1,0:T(8,128)S(1)}, u32[]{:S(2)}, u32[]{:S(2)}) %collective-permute-start.1) | collective-permute-done | bytes 1441824 | tf_op jit(solution)/shard_map/ppermute | solution.py:225
  88.7 1.1 copy-done.2
  89.8 6.0 %down_rows.1 = bf16[512,2048]{1,0:T(8,128)(2,1)} custom-call(f32[704,512]{1,0:T(8,128)} %gate_up.1.p_ref, f32[704,512]{1,0:T(8,128)} %copy-done.2, bf16[172,2048]{1,0:T(8,128)(2,1)} %get-tuple-element.12.d_ref, bf16[3,172,2048]{2,1,0:T(8,128)(2,1)} %copy-done), custom_call_target="tpu_custom_call" | custom-call | tf_op jit(solution)/shard_map/down_rows/pallas_call | solution.py:137
  95.8 4.0 %all-to-all-start.2 = ((bf16[16,32,2048]{2,1,0:T(8,128)(2,1)}), bf16[16,32,2048]{2,1,0:T(8,128)(2,1)S(1)}, u32[]{:S(2)}, u32[]{:S(2)}) async-start(bf16[16,32,2048]{2,1,0:T(8,128)(2,1)} %bitcast.13), calls=%async_computation.2 | async-start | bytes 4194304 | tf_op jit(solution)/shard_map/all_to_all | solution.py:229
  99.8 0.1 select_reduce_fusion
  99.9 0.1 copy.27
  100.0 0.1 copy.28
  100.2 0.6 pad_maximum_fusion.w_ref
  100.8 30.2 %all-to-all-done.2 = bf16[16,32,2048]{2,1,0:T(8,128)(2,1)S(1)} async-done(((bf16[16,32,2048]{2,1,0:T(8,128)(2,1)}), bf16[16,32,2048]{2,1,0:T(8,128)(2,1)S(1)}, u32[]{:S(2)}, u32[]{:S(2)}) %all-to-all-start.2) | async-done | bytes 2097184 | tf_op jit(solution)/shard_map/all_to_all | solution.py:229
  131.0 1.3 copy-done.1
  132.4 3.9 %combine.1 = bf16[16,64,128]{2,1,0:T(8,128)(2,1)} custom-call(bf16[128,512]{1,0:T(8,128)(2,1)} %pad_maximum_fusion.w_ref, bf16[512,2048]{1,0:T(8,128)(2,1)} %bitcast.11), custom_call_target="tpu_custom_call" | custom-call | tf_op jit(solution)/shard_map/combine/pallas_call | solution.py:166
  136.2 24.4 %all_to_all.20 = bf16[16,64,128]{2,1,0:T(8,128)(2,1)S(1)} all-to-all(bf16[16,64,128]{2,1,0:T(8,128)(2,1)} %combine.1), channel_id=1, replica_groups=mesh['expert'=16,'tensor_0'=16,'tensor_1'=2] {'tensor_0'}, dimensions={0} | all-to-all | bytes 524288 | tf_op jit(solution)/shard_map/all_to_all | solution.py:231
  160.6 0.6 reduce_sum.35
  (15 shorter events, 0.1 us)
Async XLA Ops:
  1.5 33.1 %all-to-all-start = ((bf16[16,64,128]{2,1,0:T(8,128)(2,1)}), bf16[16,64,128]{2,1,0:T(8,128)(2,1)S(1)}, u32[]{:S(2)}, u32[]{:S(2)}) async-start(bf16[16,64,128]{2,1,0:T(8,128)(2,1)} %broadcast_in_dim.32), calls=%async_computation | async-start | bytes 524288 | tf_op jit(solution)/shard_map/all_to_all | solution.py:201
  16.7 7.2 %copy-start.4 = (s32[64,2]{0,1:T(2,128)S(1)}, s32[64,2]{0,1:T(2,128)}, u32[]{:S(2)}) copy-start(s32[64,2]{0,1:T(2,128)} %param.7) | copy-start | bytes 1540
  21.9 24.2 %collective-permute-start = (bf16[3,172,2048]{2,1,0:T(8,128)(2,1)}, bf16[3,172,2048]{2,1,0:T(8,128)(2,1)S(1)}, u32[]{:S(2)}, u32[]{:S(2)}) collective-permute-start(bf16[3,172,2048]{2,1,0:T(8,128)(2,1)} %get-tuple-element.11), channel_id=1, source_target_pairs={{0,1},{1,0},{2,3},{3,2},{4,5},{5,4},{6,7},{7,6},{8,9},{9,8},{10,11... | collective-permute-start | bytes 6340616 | tf_op jit(solution)/shard_map/ppermute | solution.py:217
  34.6 0.7 copy-start.3
  39.1 36.1 %all-to-all-start.1 = ((bf16[16,32,2048]{2,1,0:T(8,128)(2,1)}), bf16[16,32,2048]{2,1,0:T(8,128)(2,1)}, u32[]{:S(2)}, u32[]{:S(2)}) async-start(bf16[16,32,2048]{2,1,0:T(8,128)(2,1)} %bitcast.12), calls=%async_computation.1 | async-start | bytes 4194304 | tf_op jit(solution)/shard_map/all_to_all | solution.py:221
  46.2 29.0 %copy-start = (bf16[3,172,2048]{2,1,0:T(8,128)(2,1)}, bf16[3,172,2048]{2,1,0:T(8,128)(2,1)S(1)}, u32[]{:S(2)}) copy-start(bf16[3,172,2048]{2,1,0:T(8,128)(2,1)S(1)} %collective-permute-done.og_ref.ou_ref.od_ref) | copy-start | bytes 6340612
  83.4 5.3 %collective-permute-start.1 = (f32[704,512]{1,0:T(8,128)}, f32[704,512]{1,0:T(8,128)S(1)}, u32[]{:S(2)}, u32[]{:S(2)}) collective-permute-start(f32[704,512]{1,0:T(8,128)} %gate_up.1.p_ref), channel_id=1, source_target_pairs={{0,1},{1,0},{2,3},{3,2},{4,5},{5,4},{6,7},{7,6},{8,9},{9,8},{10,11... | collective-permute-start | bytes 4325384 | tf_op jit(solution)/shard_map/ppermute | solution.py:225
  88.7 1.1 copy-start.2
  95.8 4.0 %copy-start.5 = (f32[64,2]{0,1:T(2,128)S(1)}, f32[64,2]{0,1:T(2,128)}, u32[]{:S(2)}) copy-start(f32[64,2]{0,1:T(2,128)} %param.8) | copy-start | bytes 1540
  95.8 35.3 %all-to-all-start.2 = ((bf16[16,32,2048]{2,1,0:T(8,128)(2,1)}), bf16[16,32,2048]{2,1,0:T(8,128)(2,1)S(1)}, u32[]{:S(2)}, u32[]{:S(2)}) async-start(bf16[16,32,2048]{2,1,0:T(8,128)(2,1)} %bitcast.13), calls=%async_computation.2 | async-start | bytes 4194304 | tf_op jit(solution)/shard_map/all_to_all | solution.py:229
  131.0 1.3 copy-start.1

commit v2 on v0

v2 whole, which is shorter than its diff:
```python
import jax
import jax.numpy as jnp
from jax import lax
from jax.experimental import pallas as pl
from jax.experimental.pallas import tpu as pltpu
from jax.sharding import Mesh
from jax.sharding import PartitionSpec as P

BF = jnp.bfloat16
F32 = jnp.float32
TENSOR = ("far", "near", "core")
WIDE = ("expert", "near", "core")
ANY = pl.BlockSpec(memory_space=pl.ANY)
VMEM = pl.BlockSpec(memory_space=pltpu.VMEM)


def params(mib):
    return pltpu.CompilerParams(vmem_limit_bytes=mib * 2**20)


def dispatch(select, gathered, experts, cores):
    planes, rows, lanes = gathered.shape
    slots = select.shape[0] // experts // cores
    width = planes * lanes
    per = 4
    steps = planes // per

    def kernel(s_ref, x_ref, o_ref, held, sem):
        s = s_ref[...]
        copies = []
        for k in range(steps):
            x = jnp.concatenate([x_ref[per * k + i] for i in range(per)], axis=1)
            y = jnp.dot(s, x, preferred_element_type=F32).astype(BF)
            held[k] = y.reshape(experts, cores, slots, per * lanes)
            for i in range(4):
                at = pl.ds(k * per * lanes, per * lanes)
                out = o_ref.at[:, i // 2, i % 2, :, :, at]
                copies.append(pltpu.make_async_copy(held.at[k], out, sem.at[k, i]))
                copies[-1].start()
        for copy in copies:
            copy.wait()

    return pl.pallas_call(
        kernel,
        in_specs=[VMEM] * 2,
        out_specs=ANY,
        out_shape=jax.ShapeDtypeStruct((experts, 2, 2, cores, slots, width), BF),
        scratch_shapes=[
            pltpu.VMEM((steps, experts, cores, slots, per * lanes), BF),
            pltpu.SemaphoreType.DMA((steps, 4)),
        ],
        compiler_params=params(8),
        name="dispatch",
    )(select, gathered)


def feed_forward(incoming, own, other):
    blocks, slots, width = incoming.shape
    units, features = own[0].shape
    ways = features // width
    groups = blocks // ways
    rows = groups * slots
    tall = -(-units // 16) * 16
    steps = 4
    lanes = width // steps
    span = lanes * ways
    parts = lanes // 128

    def stack(ref, step, count):
        blank = jnp.zeros((tall - units, span), BF)
        pieces = [piece for i in range(count) for piece in (ref[step, i], blank)]
        return jnp.concatenate(pieces, axis=0)

    def kernel(x_ref, g, u, d, og, ou, od, o_ref, xs, ws, ds, total, hidden, ys, sx, sw, sd, so):
        first, last = (g, og, u, ou), (d, od)
        loads = []
        for t in range(steps):
            at = pl.ds(t * span, span)
            load = [
                pltpu.make_async_copy(x_ref.at[:, :, pl.ds(t * lanes, lanes)], xs.at[t], sx.at[t])
            ]
            for i, w in enumerate(first):
                load.append(pltpu.make_async_copy(w.at[:, at], ws.at[t, i], sw.at[t, i]))
            loads.append(load)
        for t in range(steps):
            at = pl.ds(t * span, span)
            loads.append(
                [
                    pltpu.make_async_copy(w.at[:, at], ds.at[t, i], sd.at[t, i])
                    for i, w in enumerate(last)
                ]
            )
        for load in loads:
            for copy in load:
                copy.start()

        for t in range(steps):
            for copy in loads[t]:
                copy.wait()
            x = xs[t].reshape(groups, ways, slots, lanes)
            x = jnp.concatenate(
                [
                    x[:, k, :, p * 128 : (p + 1) * 128].reshape(rows, 128)
                    for p in range(parts)
                    for k in range(ways)
                ],
                axis=1,
            )
            part = lax.dot_general(
                x, stack(ws, t, 4), (((1,), (1,)), ((), ())), preferred_element_type=F32
            )
            if t == 0:
                total[...] = part
            else:
                total[...] += part
        gate, up = total[:, : 2 * tall], total[:, 2 * tall :]
        hidden[...] = (gate / (1.0 + jnp.exp(-gate)) * up).astype(BF)

        stores = []
        for t in range(steps):
            for copy in loads[steps + t]:
                copy.wait()
            y = jnp.dot(hidden[...], stack(ds, t, 2), preferred_element_type=F32).astype(BF)
            for p in range(parts):
                for k in range(ways):
                    at = (p * ways + k) * 128
                    ys[t, :, k, :, p * 128 : (p + 1) * 128] = y[:, at : at + 128].reshape(
                        groups, slots, 128
                    )
            out = o_ref.at[:, :, :, pl.ds(t * lanes, lanes)]
            stores.append(pltpu.make_async_copy(ys.at[t], out, so.at[t]))
            stores[-1].start()
        for copy in stores:
            copy.wait()

    out = pl.pallas_call(
        kernel,
        in_specs=[ANY] * 7,
        out_specs=ANY,
        out_shape=jax.ShapeDtypeStruct((groups, ways, slots, width), BF),
        scratch_shapes=[
            pltpu.VMEM((steps, blocks, slots, lanes), BF),
            pltpu.VMEM((steps, 4, units, span), BF),
            pltpu.VMEM((steps, 2, units, span), BF),
            pltpu.VMEM((rows, 4 * tall), F32),
            pltpu.VMEM((rows, 2 * tall), BF),
            pltpu.VMEM((steps, groups, ways, slots, lanes), BF),
            pltpu.SemaphoreType.DMA((steps,)),
            pltpu.SemaphoreType.DMA((steps, 4)),
            pltpu.SemaphoreType.DMA((steps, 2)),
            pltpu.SemaphoreType.DMA((steps,)),
        ],
        compiler_params=params(48),
        name="feed_forward",
    )(incoming, *own, *other)
    return out.reshape(blocks, slots, width)


def combine(weights, returned, planes):
    twice = weights.shape[0]
    rows = twice // 2
    lanes = returned.shape[1] // planes

    def kernel(w_ref, r_ref, o_ref):
        w = w_ref[...]
        for k in range(0, planes, 2):
            total = jnp.dot(w, r_ref[:, k * lanes : (k + 2) * lanes], preferred_element_type=F32)
            total = (total[:rows] + total[rows:]).astype(BF)
            o_ref[k] = total[:, :lanes]
            o_ref[k + 1] = total[:, lanes:]

    return pl.pallas_call(
        kernel,
        in_specs=[VMEM] * 2,
        out_specs=VMEM,
        out_shape=jax.ShapeDtypeStruct((planes, rows, lanes), BF),
        compiler_params=params(8),
        name="combine",
    )(weights, returned)


def slot_positions(route_block, experts, capacity):
    flat_routes = route_block.reshape(-1)
    onehot = (flat_routes[:, None] == jnp.arange(experts, dtype=jnp.int32)[None, :]).astype(
        jnp.int32
    )
    earlier = jnp.cumsum(onehot, axis=0) - onehot
    slot_index = jnp.sum(earlier * onehot, axis=1)
    return (flat_routes * capacity + slot_index).reshape(route_block.shape)


def exchange(blocks, axes):
    return lax.all_to_all(blocks, axes, split_axis=0, concat_axis=0, tiled=True)


def local(tokens, routes, route_weight, gate_weight, up_weight, down_weight):
    group_count = lax.axis_size("expert")
    planes = lax.axis_size("far")
    cores = lax.axis_size("core")
    experts = group_count // 2
    tok_rows, lanes = tokens.shape
    capacity = min(tok_rows, 4 * tok_rows // experts)
    slots_out = experts * capacity
    slots = capacity // cores
    blocks = group_count * 2 * cores
    width = planes * lanes

    gathered = exchange(jnp.broadcast_to(tokens[None], (planes, tok_rows, lanes)), "far")

    positions = slot_positions(routes, experts, capacity)
    slot_ids = jnp.arange(slots_out, dtype=jnp.int32)
    matches = positions[:, :, None] == slot_ids[None, None, :]
    select = jnp.any(matches, axis=1).astype(BF).T
    mix = jnp.sum(jnp.where(matches, route_weight[:, :, None], 0.0), axis=1)
    mix = mix.reshape(tok_rows, experts, 1, capacity)
    mix = jnp.broadcast_to(mix, (tok_rows, experts, 4, capacity)).reshape(tok_rows, 4 * slots_out)
    high = lax.reduce_precision(mix, 8, 7)
    mix = jnp.concatenate([high, mix - high], axis=0).astype(BF)

    outgoing = dispatch(select, gathered, experts, cores)
    own = (gate_weight[0], up_weight[0], down_weight[0])
    other = tuple(lax.ppermute(w, "core", [(0, 1), (1, 0)]) for w in own)
    incoming = exchange(outgoing.reshape(blocks, slots, width), WIDE)

    result = feed_forward(incoming, own, other)

    returned = exchange(result, WIDE)
    mixed = combine(mix, returned.reshape(blocks * slots, width), planes)
    mixed = exchange(mixed, "far")
    return jnp.sum(mixed.astype(F32), axis=0).astype(BF)


def solution(mesh):
    torus = Mesh(
        mesh.devices.reshape(mesh.shape["expert"], 8, 2, 2), ("expert", "far", "near", "core")
    )
    placed = (
        P("expert", TENSOR),
        P("expert", None),
        P("expert", None),
        P("expert", TENSOR, None),
        P("expert", TENSOR, None),
        P("expert", TENSOR, None),
    )
    return jax.shard_map(
        local, mesh=torus, in_specs=placed, out_specs=P("expert", TENSOR), check_vma=False
    )
```

time: 241 us -> 136 us (0.56)
  the two profiles are of different devices: /device:TPU:2 before, /device:TPU:1 now
where the time goes in v2:
time: 136 us
  waiting for transfers between devices  59.8 us (44%)
  starting transfers between devices  39.6 us (29%)
  blocking collectives  16.9 us (12%)
  Pallas kernels  9.18 us (7%)
  local copies, waits for them, and re-layouts  7.92 us (6%)
  other arithmetic  2 us (1%)
    all_to_all x3, waiting for transfers between devices, exchange(): return lax.all_to_all(blocks, axes, split_axis=0, concat_axis=0, tiled=True)  58.9 us
    all_to_all x3, starting transfers between devices, exchange(): return lax.all_to_all(blocks, axes, split_axis=0, concat_axis=0, tiled=True)  32.8 us
    all_to_all x1, blocking collectives, exchange(): return lax.all_to_all(blocks, axes, split_axis=0, concat_axis=0, tiled=True)  16.9 us
    pallas_call x1, Pallas kernels, feed_forward(): pl.pallas_call(kernel, in_specs=[ANY] * 7, out_specs=ANY, out_shape=jax.S...  7.12 us
    ppermute x3, starting transfers between devices, local(): other = tuple((lax.ppermute(w, 'core', [(0, 1), (1, 0)]) for w in own))  6.77 us
    unnamed x15, local copies, waits for them, and re-layouts  5.75 us
  transfers between devices with their start and end apart: 6, of which 4 were waited for; matrix products, arithmetic and copies ran while one was open for 2% of the time, Pallas kernels for 0%

profile of v2, /device:TPU:1, one launch (start us, length us, event | category | flops | bytes accessed | tf_op | source)
XLA Modules:
  0.0 135.6 jit_solution(811130806159201484)
XLA Ops:
  0.0 1.4 %broadcast_in_dim.32 = bf16[8,64,128]{2,1,0:T(8,128)(2,1)} broadcast(bf16[64,128]{1,0:T(8,128)(2,1)} %param.6), dimensions={1,2} | broadcast | bytes 147456 | tf_op jit(solution)/shard_map/broadcast_in_dim | solution.py:208
  1.4 15.6 %all-to-all-start = ((bf16[8,64,128]{2,1,0:T(8,128)(2,1)}), bf16[8,64,128]{2,1,0:T(8,128)(2,1)S(1)}, u32[]{:S(2)}, u32[]{:S(2)}) async-start(bf16[8,64,128]{2,1,0:T(8,128)(2,1)} %broadcast_in_dim.32), calls=%async_computation | async-start | bytes 262144 | tf_op jit(solution)/shard_map/all_to_all | solution.py:193
  17.0 0.8 copy.25
  17.8 0.1 eq.28
  17.9 0.1 fusion.2
  18.0 0.2 reduce_window_sum.11
  18.2 0.2 select_reduce_fusion.1
  18.4 0.1 reduce_sum.33
  18.6 0.7 multiply_add_fusion
  19.3 0.1 fusion.1
  19.4 0.1 copy.30
  19.5 10.7 %all-to-all-done.x_ref = bf16[8,64,128]{2,1,0:T(8,128)(2,1)S(1)} async-done(((bf16[8,64,128]{2,1,0:T(8,128)(2,1)}), bf16[8,64,128]{2,1,0:T(8,128)(2,1)S(1)}, u32[]{:S(2)}, u32[]{:S(2)}) %all-to-all-start) | async-done | bytes 131104 | tf_op jit(solution)/shard_map/all_to_all | solution.py:193
  30.2 1.6 %dispatch.1 = bf16[8,2,2,2,16,1024]{5,4,3,2,1,0:T(8,128)(2,1)} custom-call(bf16[256,64]{1,0:T(8,128)(2,1)S(1)} %bitcast.16, bf16[8,64,128]{2,1,0:T(8,128)(2,1)S(1)} %all-to-all-done.x_ref), custom_call_target="tpu_custom_call" | custom-call | tf_op jit(solution)/shard_map/dispatch/pallas_call | solution.py:43
  31.8 12.0 %all-to-all-start.1 = ((bf16[64,16,1024]{2,1,0:T(8,128)(2,1)}), bf16[64,16,1024]{2,1,0:T(8,128)(2,1)}, u32[]{:S(2)}, u32[]{:S(2)}) async-start(bf16[64,16,1024]{2,1,0:T(8,128)(2,1)} %bitcast.3), calls=%async_computation.1 | async-start | bytes 4194304 | tf_op jit(solution)/shard_map/all_to_all | solution.py:193
  43.8 2.4 %collective-permute-start = (bf16[172,4096]{1,0:T(8,128)(2,1)S(1)}, bf16[172,4096]{1,0:T(8,128)(2,1)S(1)}, u32[]{:S(2)}, u32[]{:S(2)}) collective-permute-start(bf16[172,4096]{1,0:T(8,128)(2,1)S(1)} %bitcast.10), channel_id=1, source_target_pairs={{0,1},{1,0},{2,3},{3,2},{4,5},{5,4},{6,7},{7,6},{8,9},{9,8},{10,11... | collective-permute-start | bytes 4227080 | tf_op jit(solution)/shard_map/ppermute | solution.py:222
  46.3 1.9 %collective-permute-start.1 = (bf16[172,4096]{1,0:T(8,128)(2,1)S(1)}, bf16[172,4096]{1,0:T(8,128)(2,1)S(1)}, u32[]{:S(2)}, u32[]{:S(2)}) collective-permute-start(bf16[172,4096]{1,0:T(8,128)(2,1)S(1)} %bitcast.12), channel_id=1, source_target_pairs={{0,1},{1,0},{2,3},{3,2},{4,5},{5,4},{6,7},{7,6},{8,9},{9,8},{10,11... | collective-permute-start | bytes 4227080 | tf_op jit(solution)/shard_map/ppermute | solution.py:222
  48.2 2.4 %collective-permute-start.2 = (bf16[172,4096]{1,0:T(8,128)(2,1)}, bf16[172,4096]{1,0:T(8,128)(2,1)}, u32[]{:S(2)}, u32[]{:S(2)}) collective-permute-start(bf16[172,4096]{1,0:T(8,128)(2,1)} %bitcast.14), channel_id=1, source_target_pairs={{0,1},{1,0},{2,3},{3,2},{4,5},{5,4},{6,7},{7,6},{8,9},{9,8},{10,11... | collective-permute-start | bytes 4227080 | tf_op jit(solution)/shard_map/ppermute | solution.py:222
  50.7 1.1 copy-done.3
  51.8 1.1 copy-done.5
  52.9 0.9 collective-permute-done.2.od
  53.8 19.3 %all-to-all-done.1.x_ref = bf16[64,16,1024]{2,1,0:T(8,128)(2,1)} async-done(((bf16[64,16,1024]{2,1,0:T(8,128)(2,1)}), bf16[64,16,1024]{2,1,0:T(8,128)(2,1)}, u32[]{:S(2)}, u32[]{:S(2)}) %all-to-all-start.1) | async-done | bytes 2097184 | tf_op jit(solution)/shard_map/all_to_all | solution.py:193
  73.2 1.4 %copy-done.2 = bf16[1,172,4096]{2,1,0:T(8,128)(2,1)S(1)} copy-done((bf16[1,172,4096]{2,1,0:T(8,128)(2,1)S(1)}, bf16[1,172,4096]{2,1,0:T(8,128)(2,1)}, u32[]{:S(2)}) %copy-start.2) | copy-done | bytes 1409048
  74.5 1.4 %copy-done.4 = bf16[172,4096]{1,0:T(8,128)(2,1)S(1)} copy-done((bf16[172,4096]{1,0:T(8,128)(2,1)S(1)}, bf16[172,4096]{1,0:T(8,128)(2,1)}, u32[]{:S(2)}) %copy-start.4) | copy-done | bytes 1409048
  75.9 7.1 %feed_forward.1 = bf16[16,4,16,1024]{3,2,1,0:T(8,128)(2,1)} custom-call(bf16[64,16,1024]{2,1,0:T(8,128)(2,1)} %all-to-all-done.1.x_ref, bf16[172,4096]{1,0:T(8,128)(2,1)S(1)} %bitcast.11, bf16[172,4096]{1,0:T(8,128)(2,1)S(1)} %bitcast.13, bf16[172,4096]{1,0:T(8,128)(2,1)S(1)} %bitcast.15, bf16[172,4096]{1,0:T(8,128)(2,1)S(1)} %copy-done.4, ...), custom_call_target="tpu_custom_call" | custom-call | tf_op jit(solution)/shard_map/feed_forward/pallas_call | solution.py:136
  83.0 5.2 %all-to-all-start.2 = ((bf16[64,16,1024]{2,1,0:T(8,128)(2,1)}), bf16[64,16,1024]{2,1,0:T(8,128)(2,1)S(1)}, u32[]{:S(2)}, u32[]{:S(2)}) async-start(bf16[64,16,1024]{2,1,0:T(8,128)(2,1)} %bitcast.17), calls=%async_computation.2 | async-start | bytes 4194304 | tf_op jit(solution)/shard_map/all_to_all | solution.py:193
  88.2 0.1 select_reduce_fusion
  88.3 0.1 copy.27
  88.5 0.2 copy.28
  88.8 28.9 %all-to-all-done.2 = bf16[64,16,1024]{2,1,0:T(8,128)(2,1)S(1)} async-done(((bf16[64,16,1024]{2,1,0:T(8,128)(2,1)}), bf16[64,16,1024]{2,1,0:T(8,128)(2,1)S(1)}, u32[]{:S(2)}, u32[]{:S(2)}) %all-to-all-start.2) | async-done | bytes 2097184 | tf_op jit(solution)/shard_map/all_to_all | solution.py:193
  117.6 0.5 combine.1
  118.1 16.9 %all_to_all.20 = bf16[8,64,128]{2,1,0:T(8,128)(2,1)S(1)} all-to-all(bf16[8,64,128]{2,1,0:T(8,128)(2,1)S(1)} %combine.1), channel_id=1, replica_groups=mesh['expert'=16,'far'=8,'near'=2,'core'=2] {'far'}, dimensions={0} | all-to-all | bytes 262144 | tf_op jit(solution)/shard_map/all_to_all | solution.py:193
  135.0 0.6 reduce_sum.35
  (17 shorter events, 0.2 us)
Async XLA Ops:
  1.4 28.8 %all-to-all-start = ((bf16[8,64,128]{2,1,0:T(8,128)(2,1)}), bf16[8,64,128]{2,1,0:T(8,128)(2,1)S(1)}, u32[]{:S(2)}, u32[]{:S(2)}) async-start(bf16[8,64,128]{2,1,0:T(8,128)(2,1)} %broadcast_in_dim.32), calls=%async_computation | async-start | bytes 262144 | tf_op jit(solution)/shard_map/all_to_all | solution.py:193
  31.8 12.0 %copy-start = (bf16[1,172,4096]{2,1,0:T(8,128)(2,1)S(1)}, bf16[1,172,4096]{2,1,0:T(8,128)(2,1)}, u32[]{:S(2)}) copy-start(bf16[1,172,4096]{2,1,0:T(8,128)(2,1)} %param.9) | copy-start | bytes 4227076
  31.8 14.5 %copy-start.1 = (bf16[1,172,4096]{2,1,0:T(8,128)(2,1)S(1)}, bf16[1,172,4096]{2,1,0:T(8,128)(2,1)}, u32[]{:S(2)}) copy-start(bf16[1,172,4096]{2,1,0:T(8,128)(2,1)} %param.10) | copy-start | bytes 4227076
  31.8 41.3 %all-to-all-start.1 = ((bf16[64,16,1024]{2,1,0:T(8,128)(2,1)}), bf16[64,16,1024]{2,1,0:T(8,128)(2,1)}, u32[]{:S(2)}, u32[]{:S(2)}) async-start(bf16[64,16,1024]{2,1,0:T(8,128)(2,1)} %bitcast.3), calls=%async_computation.1 | async-start | bytes 4194304 | tf_op jit(solution)/shard_map/all_to_all | solution.py:193
  43.8 6.8 %collective-permute-start = (bf16[172,4096]{1,0:T(8,128)(2,1)S(1)}, bf16[172,4096]{1,0:T(8,128)(2,1)S(1)}, u32[]{:S(2)}, u32[]{:S(2)}) collective-permute-start(bf16[172,4096]{1,0:T(8,128)(2,1)S(1)} %bitcast.10), channel_id=1, source_target_pairs={{0,1},{1,0},{2,3},{3,2},{4,5},{5,4},{6,7},{7,6},{8,9},{9,8},{10,11... | collective-permute-start | bytes 4227080 | tf_op jit(solution)/shard_map/ppermute | solution.py:222
  46.3 5.5 %collective-permute-start.1 = (bf16[172,4096]{1,0:T(8,128)(2,1)S(1)}, bf16[172,4096]{1,0:T(8,128)(2,1)S(1)}, u32[]{:S(2)}, u32[]{:S(2)}) collective-permute-start(bf16[172,4096]{1,0:T(8,128)(2,1)S(1)} %bitcast.12), channel_id=1, source_target_pairs={{0,1},{1,0},{2,3},{3,2},{4,5},{5,4},{6,7},{7,6},{8,9},{9,8},{10,11... | collective-permute-start | bytes 4227080 | tf_op jit(solution)/shard_map/ppermute | solution.py:222
  48.2 5.6 %collective-permute-start.2 = (bf16[172,4096]{1,0:T(8,128)(2,1)}, bf16[172,4096]{1,0:T(8,128)(2,1)}, u32[]{:S(2)}, u32[]{:S(2)}) collective-permute-start(bf16[172,4096]{1,0:T(8,128)(2,1)} %bitcast.14), channel_id=1, source_target_pairs={{0,1},{1,0},{2,3},{3,2},{4,5},{5,4},{6,7},{7,6},{8,9},{9,8},{10,11... | collective-permute-start | bytes 4227080 | tf_op jit(solution)/shard_map/ppermute | solution.py:222
  50.7 1.1 copy-start.3
  51.8 1.1 copy-start.5
  73.2 1.4 %copy-start.2 = (bf16[1,172,4096]{2,1,0:T(8,128)(2,1)S(1)}, bf16[1,172,4096]{2,1,0:T(8,128)(2,1)}, u32[]{:S(2)}) copy-start(bf16[1,172,4096]{2,1,0:T(8,128)(2,1)} %param.11) | copy-start | bytes 4227076
  74.5 1.4 %copy-start.4 = (bf16[172,4096]{1,0:T(8,128)(2,1)S(1)}, bf16[172,4096]{1,0:T(8,128)(2,1)}, u32[]{:S(2)}) copy-start(bf16[172,4096]{1,0:T(8,128)(2,1)} %copy-done.3) | copy-start | bytes 4227076
  83.0 5.2 %copy-start.6 = (f32[64,2]{0,1:T(2,128)S(1)}, f32[64,2]{0,1:T(2,128)}, u32[]{:S(2)}) copy-start(f32[64,2]{0,1:T(2,128)} %param.8) | copy-start | bytes 1540
  83.0 34.6 %all-to-all-start.2 = ((bf16[64,16,1024]{2,1,0:T(8,128)(2,1)}), bf16[64,16,1024]{2,1,0:T(8,128)(2,1)S(1)}, u32[]{:S(2)}, u32[]{:S(2)}) async-start(bf16[64,16,1024]{2,1,0:T(8,128)(2,1)} %bitcast.17), calls=%async_computation.2 | async-start | bytes 4194304 | tf_op jit(solution)/shard_map/all_to_all | solution.py:193

commit v3 on v2

--- a/solution.py
+++ b/solution.py
@@ -54,42 +54,63 @@
     )(select, gathered)
 
 
-def feed_forward(incoming, own, other):
+def stack_weights(own, other):
+    units, features = own[0].shape
+    tall = -(-units // 16) * 16
+    span = features // 4
+
+    def kernel(g, u, d, og, ou, od, first_ref, last_ref):
+        blank = jnp.zeros((tall - units, span), BF)
+        for i, src in enumerate((g, og, u, ou)):
+            first_ref[i * tall : (i + 1) * tall] = jnp.concatenate([src[...], blank], axis=0)
+        for i, src in enumerate((d, od)):
+            last_ref[i * tall : (i + 1) * tall] = jnp.concatenate([src[...], blank], axis=0)
+
+    def columns(rows):
+        return pl.BlockSpec((rows, span), lambda i: (0, i))
+
+    return pl.pallas_call(
+        kernel,
+        grid=(4,),
+        in_specs=[columns(units)] * 6,
+        out_specs=[columns(4 * tall), columns(2 * tall)],
+        out_shape=[
+            jax.ShapeDtypeStruct((4 * tall, features), BF),
+            jax.ShapeDtypeStruct((2 * tall, features), BF),
+        ],
+        compiler_params=params(63),
+        name="stack_weights",
+        cost_estimate=pl.CostEstimate(
+            flops=0, bytes_accessed=24 * units * features, transcendentals=0
+        ),
+    )(*own, *other)
+
+
+def feed_forward(incoming, first, last):
     blocks, slots, width = incoming.shape
-    units, features = own[0].shape
+    tall, features = last.shape
     ways = features // width
     groups = blocks // ways
     rows = groups * slots
-    tall = -(-units // 16) * 16
     steps = 4
     lanes = width // steps
     span = lanes * ways
     parts = lanes // 128
 
-    def stack(ref, step, count):
-        blank = jnp.zeros((tall - units, span), BF)
-        pieces = [piece for i in range(count) for piece in (ref[step, i], blank)]
-        return jnp.concatenate(pieces, axis=0)
-
-    def kernel(x_ref, g, u, d, og, ou, od, o_ref, xs, ws, ds, total, hidden, ys, sx, sw, sd, so):
-        first, last = (g, og, u, ou), (d, od)
+    def kernel(x_ref, f_ref, l_ref, o_ref, xs, ws, ds, total, hidden, ys, sx, sw, sd, so):
         loads = []
         for t in range(steps):
             at = pl.ds(t * span, span)
-            load = [
-                pltpu.make_async_copy(x_ref.at[:, :, pl.ds(t * lanes, lanes)], xs.at[t], sx.at[t])
-            ]
-            for i, w in enumerate(first):
-                load.append(pltpu.make_async_copy(w.at[:, at], ws.at[t, i], sw.at[t, i]))
-            loads.append(load)
-        for t in range(steps):
-            at = pl.ds(t * span, span)
+            x_at = x_ref.at[:, :, pl.ds(t * lanes, lanes)]
             loads.append(
                 [
-                    pltpu.make_async_copy(w.at[:, at], ds.at[t, i], sd.at[t, i])
-                    for i, w in enumerate(last)
+                    pltpu.make_async_copy(x_at, xs.at[t], sx.at[t]),
+                    pltpu.make_async_copy(f_ref.at[:, at], ws.at[t], sw.at[t]),
                 ]
             )
+        for t in range(steps):
+            at = pl.ds(t * span, span)
+            loads.append([pltpu.make_async_copy(l_ref.at[:, at], ds.at[t], sd.at[t])])
         for load in loads:
             for copy in load:
                 copy.start()
@@ -107,20 +128,20 @@
                 axis=1,
             )
             part = lax.dot_general(
-                x, stack(ws, t, 4), (((1,), (1,)), ((), ())), preferred_element_type=F32
+                x, ws[t], (((1,), (1,)), ((), ())), preferred_element_type=F32
             )
             if t == 0:
                 total[...] = part
             else:
                 total[...] += part
-        gate, up = total[:, : 2 * tall], total[:, 2 * tall :]
+        gate, up = total[:, :tall], total[:, tall:]
         hidden[...] = (gate / (1.0 + jnp.exp(-gate)) * up).astype(BF)
 
         stores = []
         for t in range(steps):
             for copy in loads[steps + t]:
                 copy.wait()
-            y = jnp.dot(hidden[...], stack(ds, t, 2), preferred_element_type=F32).astype(BF)
+            y = jnp.dot(hidden[...], ds[t], preferred_element_type=F32).astype(BF)
             for p in range(parts):
                 for k in range(ways):
                     at = (p * ways + k) * 128
@@ -135,24 +156,24 @@
 
     out = pl.pallas_call(
         kernel,
-        in_specs=[ANY] * 7,
+        in_specs=[ANY] * 3,
         out_specs=ANY,
         out_shape=jax.ShapeDtypeStruct((groups, ways, slots, width), BF),
         scratch_shapes=[
             pltpu.VMEM((steps, blocks, slots, lanes), BF),
-            pltpu.VMEM((steps, 4, units, span), BF),
-            pltpu.VMEM((steps, 2, units, span), BF),
-            pltpu.VMEM((rows, 4 * tall), F32),
-            pltpu.VMEM((rows, 2 * tall), BF),
+            pltpu.VMEM((steps, 2 * tall, span), BF),
+            pltpu.VMEM((steps, tall, span), BF),
+            pltpu.VMEM((rows, 2 * tall), F32),
+            pltpu.VMEM((rows, tall), BF),
             pltpu.VMEM((steps, groups, ways, slots, lanes), BF),
             pltpu.SemaphoreType.DMA((steps,)),
-            pltpu.SemaphoreType.DMA((steps, 4)),
-            pltpu.SemaphoreType.DMA((steps, 2)),
+            pltpu.SemaphoreType.DMA((steps,)),
+            pltpu.SemaphoreType.DMA((steps,)),
             pltpu.SemaphoreType.DMA((steps,)),
         ],
-        compiler_params=params(48),
+        compiler_params=params(63),
         name="feed_forward",
-    )(incoming, *own, *other)
+    )(incoming, first, last)
     return out.reshape(blocks, slots, width)
 
 
@@ -221,8 +242,9 @@
     own = (gate_weight[0], up_weight[0], down_weight[0])
     other = tuple(lax.ppermute(w, "core", [(0, 1), (1, 0)]) for w in own)
     incoming = exchange(outgoing.reshape(blocks, slots, width), WIDE)
-
-    result = feed_forward(incoming, own, other)
+    first, last = stack_weights(own, other)
+
+    result = feed_forward(incoming, first, last)
 
     returned = exchange(result, WIDE)
     mixed = combine(mix, returned.reshape(blocks * slots, width), planes)

time: 136 us -> 134 us (0.985)
  Pallas kernels: 9.18 us -> 16.7 us
  waiting for transfers between devices: 59.8 us -> 53.4 us
  local copies, waits for them, and re-layouts: 7.92 us -> 4.42 us
    pallas_call x1 -> x2, Pallas kernels: 7.12 us -> 14.6 us  [the longest x1 7.5 us: feed_forward(): pl.pallas_call(kernel, in_specs=[ANY] * 3, out_specs=ANY, out_shape=jax.S...]
    all_to_all x3, waiting for transfers between devices: 58.9 us -> 51.8 us  [exchange(): return lax.all_to_all(blocks, axes, split_axis=0, concat_axis=0, tiled=True)]
    unnamed x15 -> x11, local copies, waits for them, and re-layouts: 5.75 us -> 2.26 us
  transfers between devices with their start and end apart: 6 -> 6, of which waited for: 4 -> 5; matrix products, arithmetic and copies ran while one was open for 2% -> 2% of each run, Pallas kernels for 0% -> 5%
where the time goes in v3:
time: 134 us; the launch traced here: 133 us
  waiting for transfers between devices  53.4 us (40%)
  starting transfers between devices  39.6 us (30%)
  blocking collectives  16.9 us (13%)
  Pallas kernels  16.7 us (12%)
  local copies, waits for them, and re-layouts  4.42 us (3%)
  other arithmetic  2 us (1%)
    all_to_all x3, waiting for transfers between devices, exchange(): return lax.all_to_all(blocks, axes, split_axis=0, concat_axis=0, tiled=True)  51.8 us
    all_to_all x3, starting transfers between devices, exchange(): return lax.all_to_all(blocks, axes, split_axis=0, concat_axis=0, tiled=True)  32.8 us
    all_to_all x1, blocking collectives, exchange(): return lax.all_to_all(blocks, axes, split_axis=0, concat_axis=0, tiled=True)  16.9 us
    pallas_call x1, Pallas kernels, feed_forward(): pl.pallas_call(kernel, in_specs=[ANY] * 3, out_specs=ANY, out_shape=jax.S...  7.5 us
    pallas_call x1, Pallas kernels, stack_weights(): pl.pallas_call(kernel, grid=(4,), in_specs=[columns(units)] * 6, out_spec...  7.13 us
    ppermute x3, starting transfers between devices, local(): other = tuple((lax.ppermute(w, 'core', [(0, 1), (1, 0)]) for w in own))  6.77 us
  transfers between devices with their start and end apart: 6, of which 5 were waited for; matrix products, arithmetic and copies ran while one was open for 2% of the time, Pallas kernels for 5%

profile of v3, /device:TPU:1, one launch (start us, length us, event | category | flops | bytes accessed | tf_op | source)
XLA Modules:
  0.0 133.2 jit_solution(3955336209744963866)
XLA Ops:
  0.0 1.4 %broadcast_in_dim.32 = bf16[8,64,128]{2,1,0:T(8,128)(2,1)} broadcast(bf16[64,128]{1,0:T(8,128)(2,1)} %param.6), dimensions={1,2} | broadcast | bytes 147456 | tf_op jit(solution)/shard_map/broadcast_in_dim | solution.py:229
  1.4 15.6 %all-to-all-start = ((bf16[8,64,128]{2,1,0:T(8,128)(2,1)}), bf16[8,64,128]{2,1,0:T(8,128)(2,1)S(1)}, u32[]{:S(2)}, u32[]{:S(2)}) async-start(bf16[8,64,128]{2,1,0:T(8,128)(2,1)} %broadcast_in_dim.32), calls=%async_computation | async-start | bytes 262144 | tf_op jit(solution)/shard_map/all_to_all | solution.py:214
  17.0 0.8 copy.25
  17.8 0.1 eq.28
  17.9 0.1 fusion.2
  18.0 0.2 reduce_window_sum.11
  18.2 0.2 select_reduce_fusion.1
  18.3 0.1 reduce_sum.33
  18.6 0.7 multiply_add_fusion
  19.3 0.1 fusion.1
  19.4 0.1 copy.30
  19.5 10.7 %all-to-all-done.x_ref = bf16[8,64,128]{2,1,0:T(8,128)(2,1)S(1)} async-done(((bf16[8,64,128]{2,1,0:T(8,128)(2,1)}), bf16[8,64,128]{2,1,0:T(8,128)(2,1)S(1)}, u32[]{:S(2)}, u32[]{:S(2)}) %all-to-all-start) | async-done | bytes 131104 | tf_op jit(solution)/shard_map/all_to_all | solution.py:214
  30.2 1.6 %dispatch.1 = bf16[8,2,2,2,16,1024]{5,4,3,2,1,0:T(8,128)(2,1)} custom-call(bf16[256,64]{1,0:T(8,128)(2,1)S(1)} %bitcast.10, bf16[8,64,128]{2,1,0:T(8,128)(2,1)S(1)} %all-to-all-done.x_ref), custom_call_target="tpu_custom_call" | custom-call | tf_op jit(solution)/shard_map/dispatch/pallas_call | solution.py:43
  31.8 12.0 %all-to-all-start.1 = ((bf16[64,16,1024]{2,1,0:T(8,128)(2,1)}), bf16[64,16,1024]{2,1,0:T(8,128)(2,1)}, u32[]{:S(2)}, u32[]{:S(2)}) async-start(bf16[64,16,1024]{2,1,0:T(8,128)(2,1)} %bitcast.3), calls=%async_computation.1 | async-start | bytes 4194304 | tf_op jit(solution)/shard_map/all_to_all | solution.py:214
  43.8 2.4 %collective-permute-start = (bf16[172,4096]{1,0:T(8,128)(2,1)S(1)}, bf16[172,4096]{1,0:T(8,128)(2,1)S(1)}, u32[]{:S(2)}, u32[]{:S(2)}) collective-permute-start(bf16[172,4096]{1,0:T(8,128)(2,1)S(1)} %bitcast.14), channel_id=1, source_target_pairs={{0,1},{1,0},{2,3},{3,2},{4,5},{5,4},{6,7},{7,6},{8,9},{9,8},{10,11... | collective-permute-start | bytes 4227080 | tf_op jit(solution)/shard_map/ppermute | solution.py:243
  46.3 1.9 %collective-permute-start.1 = (bf16[172,4096]{1,0:T(8,128)(2,1)S(1)}, bf16[172,4096]{1,0:T(8,128)(2,1)S(1)}, u32[]{:S(2)}, u32[]{:S(2)}) collective-permute-start(bf16[172,4096]{1,0:T(8,128)(2,1)S(1)} %bitcast.16), channel_id=1, source_target_pairs={{0,1},{1,0},{2,3},{3,2},{4,5},{5,4},{6,7},{7,6},{8,9},{9,8},{10,11... | collective-permute-start | bytes 4227080 | tf_op jit(solution)/shard_map/ppermute | solution.py:243
  48.2 2.4 %collective-permute-start.2 = (bf16[172,4096]{1,0:T(8,128)(2,1)}, bf16[172,4096]{1,0:T(8,128)(2,1)}, u32[]{:S(2)}, u32[]{:S(2)}) collective-permute-start(bf16[172,4096]{1,0:T(8,128)(2,1)} %bitcast.17), channel_id=1, source_target_pairs={{0,1},{1,0},{2,3},{3,2},{4,5},{5,4},{6,7},{7,6},{8,9},{9,8},{10,11... | collective-permute-start | bytes 4227080 | tf_op jit(solution)/shard_map/ppermute | solution.py:243
  50.6 0.8 collective-permute-done.1.ou
  51.4 0.4 copy-done.2
  51.8 1.1 copy-done.3
  52.9 0.9 collective-permute-done.2.od
  53.8 7.1 %stack_weights.1 = (bf16[704,4096]{1,0:T(8,128)(2,1)}, bf16[352,4096]{1,0:T(8,128)(2,1)}) custom-call(bf16[172,4096]{1,0:T(8,128)(2,1)} %bitcast.13, bf16[172,4096]{1,0:T(8,128)(2,1)} %bitcast.15, bf16[172,4096]{1,0:T(8,128)(2,1)} %bitcast.18, bf16[172,4096]{1,0:T(8,128)(2,1)} %copy-done.2, bf16[172,4096]{1,0:T(8,128)(2,1)} %copy-done.3, ...), custom_call_target="tpu_custom_call" | custom-call | bytes 16908288 | tf_op jit(solution)/shard_map/stack_weights/pallas_call | solution.py:72
  60.9 12.2 %all-to-all-done.1.x_ref = bf16[64,16,1024]{2,1,0:T(8,128)(2,1)} async-done(((bf16[64,16,1024]{2,1,0:T(8,128)(2,1)}), bf16[64,16,1024]{2,1,0:T(8,128)(2,1)}, u32[]{:S(2)}, u32[]{:S(2)}) %all-to-all-start.1) | async-done | bytes 2097184 | tf_op jit(solution)/shard_map/all_to_all | solution.py:214
  73.1 7.5 %feed_forward.1 = bf16[16,4,16,1024]{3,2,1,0:T(8,128)(2,1)} custom-call(bf16[64,16,1024]{2,1,0:T(8,128)(2,1)} %all-to-all-done.1.x_ref, bf16[704,4096]{1,0:T(8,128)(2,1)} %get-tuple-element.7.f_ref, bf16[352,4096]{1,0:T(8,128)(2,1)} %get-tuple-element.8.l_ref), custom_call_target="tpu_custom_call" | custom-call | tf_op jit(solution)/shard_map/feed_forward/pallas_call | solution.py:157
  80.7 5.2 %all-to-all-start.2 = ((bf16[64,16,1024]{2,1,0:T(8,128)(2,1)}), bf16[64,16,1024]{2,1,0:T(8,128)(2,1)S(1)}, u32[]{:S(2)}, u32[]{:S(2)}) async-start(bf16[64,16,1024]{2,1,0:T(8,128)(2,1)} %bitcast.11), calls=%async_computation.2 | async-start | bytes 4194304 | tf_op jit(solution)/shard_map/all_to_all | solution.py:214
  85.9 0.1 select_reduce_fusion
  86.0 0.1 copy.27
  86.1 0.2 copy.28
  86.4 28.9 %all-to-all-done.2 = bf16[64,16,1024]{2,1,0:T(8,128)(2,1)S(1)} async-done(((bf16[64,16,1024]{2,1,0:T(8,128)(2,1)}), bf16[64,16,1024]{2,1,0:T(8,128)(2,1)S(1)}, u32[]{:S(2)}, u32[]{:S(2)}) %all-to-all-start.2) | async-done | bytes 2097184 | tf_op jit(solution)/shard_map/all_to_all | solution.py:214
  115.3 0.4 combine.1
  115.7 16.9 %all_to_all.20 = bf16[8,64,128]{2,1,0:T(8,128)(2,1)S(1)} all-to-all(bf16[8,64,128]{2,1,0:T(8,128)(2,1)S(1)} %combine.1), channel_id=1, replica_groups=mesh['expert'=16,'far'=8,'near'=2,'core'=2] {'far'}, dimensions={0} | all-to-all | bytes 262144 | tf_op jit(solution)/shard_map/all_to_all | solution.py:214
  132.6 0.6 reduce_sum.35
  (14 shorter events, 0.2 us)
Async XLA Ops:
  1.4 28.8 %all-to-all-start = ((bf16[8,64,128]{2,1,0:T(8,128)(2,1)}), bf16[8,64,128]{2,1,0:T(8,128)(2,1)S(1)}, u32[]{:S(2)}, u32[]{:S(2)}) async-start(bf16[8,64,128]{2,1,0:T(8,128)(2,1)} %broadcast_in_dim.32), calls=%async_computation | async-start | bytes 262144 | tf_op jit(solution)/shard_map/all_to_all | solution.py:214
  31.8 12.0 %copy-start = (bf16[1,172,4096]{2,1,0:T(8,128)(2,1)S(1)}, bf16[1,172,4096]{2,1,0:T(8,128)(2,1)}, u32[]{:S(2)}) copy-start(bf16[1,172,4096]{2,1,0:T(8,128)(2,1)} %param.9) | copy-start | bytes 4227076
  31.8 14.5 %copy-start.1 = (bf16[1,172,4096]{2,1,0:T(8,128)(2,1)S(1)}, bf16[1,172,4096]{2,1,0:T(8,128)(2,1)}, u32[]{:S(2)}) copy-start(bf16[1,172,4096]{2,1,0:T(8,128)(2,1)} %param.10) | copy-start | bytes 4227076
  31.8 41.3 %all-to-all-start.1 = ((bf16[64,16,1024]{2,1,0:T(8,128)(2,1)}), bf16[64,16,1024]{2,1,0:T(8,128)(2,1)}, u32[]{:S(2)}, u32[]{:S(2)}) async-start(bf16[64,16,1024]{2,1,0:T(8,128)(2,1)} %bitcast.3), calls=%async_computation.1 | async-start | bytes 4194304 | tf_op jit(solution)/shard_map/all_to_all | solution.py:214
  43.8 6.8 %collective-permute-start = (bf16[172,4096]{1,0:T(8,128)(2,1)S(1)}, bf16[172,4096]{1,0:T(8,128)(2,1)S(1)}, u32[]{:S(2)}, u32[]{:S(2)}) collective-permute-start(bf16[172,4096]{1,0:T(8,128)(2,1)S(1)} %bitcast.14), channel_id=1, source_target_pairs={{0,1},{1,0},{2,3},{3,2},{4,5},{5,4},{6,7},{7,6},{8,9},{9,8},{10,11... | collective-permute-start | bytes 4227080 | tf_op jit(solution)/shard_map/ppermute | solution.py:243
  46.3 5.1 %collective-permute-start.1 = (bf16[172,4096]{1,0:T(8,128)(2,1)S(1)}, bf16[172,4096]{1,0:T(8,128)(2,1)S(1)}, u32[]{:S(2)}, u32[]{:S(2)}) collective-permute-start(bf16[172,4096]{1,0:T(8,128)(2,1)S(1)} %bitcast.16), channel_id=1, source_target_pairs={{0,1},{1,0},{2,3},{3,2},{4,5},{5,4},{6,7},{7,6},{8,9},{9,8},{10,11... | collective-permute-start | bytes 4227080 | tf_op jit(solution)/shard_map/ppermute | solution.py:243
  48.2 5.6 %collective-permute-start.2 = (bf16[172,4096]{1,0:T(8,128)(2,1)}, bf16[172,4096]{1,0:T(8,128)(2,1)}, u32[]{:S(2)}, u32[]{:S(2)}) collective-permute-start(bf16[172,4096]{1,0:T(8,128)(2,1)} %bitcast.17), channel_id=1, source_target_pairs={{0,1},{1,0},{2,3},{3,2},{4,5},{5,4},{6,7},{7,6},{8,9},{9,8},{10,11... | collective-permute-start | bytes 4227080 | tf_op jit(solution)/shard_map/ppermute | solution.py:243
  50.6 1.1 copy-start.2
  51.8 1.1 copy-start.3
  80.6 5.2 %copy-start.4 = (f32[64,2]{0,1:T(2,128)S(1)}, f32[64,2]{0,1:T(2,128)}, u32[]{:S(2)}) copy-start(f32[64,2]{0,1:T(2,128)} %param.8) | copy-start | bytes 1540
  80.7 34.6 %all-to-all-start.2 = ((bf16[64,16,1024]{2,1,0:T(8,128)(2,1)}), bf16[64,16,1024]{2,1,0:T(8,128)(2,1)S(1)}, u32[]{:S(2)}, u32[]{:S(2)}) async-start(bf16[64,16,1024]{2,1,0:T(8,128)(2,1)} %bitcast.11), calls=%async_computation.2 | async-start | bytes 4194304 | tf_op jit(solution)/shard_map/all_to_all | solution.py:214

commit v4 on v3

--- a/solution.py
+++ b/solution.py
@@ -96,6 +96,7 @@
     lanes = width // steps
     span = lanes * ways
     parts = lanes // 128
+    halves = 2
 
     def kernel(x_ref, f_ref, l_ref, o_ref, xs, ws, ds, total, hidden, ys, sx, sw, sd, so):
         loads = []
@@ -108,8 +109,8 @@
                     pltpu.make_async_copy(f_ref.at[:, at], ws.at[t], sw.at[t]),
                 ]
             )
-        for t in range(steps):
-            at = pl.ds(t * span, span)
+        for t in range(halves):
+            at = pl.ds(t * features // halves, features // halves)
             loads.append([pltpu.make_async_copy(l_ref.at[:, at], ds.at[t], sd.at[t])])
         for load in loads:
             for copy in load:
@@ -138,17 +139,17 @@
         hidden[...] = (gate / (1.0 + jnp.exp(-gate)) * up).astype(BF)
 
         stores = []
-        for t in range(steps):
+        for t in range(halves):
             for copy in loads[steps + t]:
                 copy.wait()
             y = jnp.dot(hidden[...], ds[t], preferred_element_type=F32).astype(BF)
-            for p in range(parts):
+            for p in range(width // halves // 128):
                 for k in range(ways):
                     at = (p * ways + k) * 128
                     ys[t, :, k, :, p * 128 : (p + 1) * 128] = y[:, at : at + 128].reshape(
                         groups, slots, 128
                     )
-            out = o_ref.at[:, :, :, pl.ds(t * lanes, lanes)]
+            out = o_ref.at[:, :, :, pl.ds(t * width // halves, width // halves)]
             stores.append(pltpu.make_async_copy(ys.at[t], out, so.at[t]))
             stores[-1].start()
         for copy in stores:
@@ -162,14 +163,14 @@
         scratch_shapes=[
             pltpu.VMEM((steps, blocks, slots, lanes), BF),
             pltpu.VMEM((steps, 2 * tall, span), BF),
-            pltpu.VMEM((steps, tall, span), BF),
+            pltpu.VMEM((halves, tall, features // halves), BF),
             pltpu.VMEM((rows, 2 * tall), F32),
             pltpu.VMEM((rows, tall), BF),
-            pltpu.VMEM((steps, groups, ways, slots, lanes), BF),
+            pltpu.VMEM((halves, groups, ways, slots, width // halves), BF),
             pltpu.SemaphoreType.DMA((steps,)),
             pltpu.SemaphoreType.DMA((steps,)),
-            pltpu.SemaphoreType.DMA((steps,)),
-            pltpu.SemaphoreType.DMA((steps,)),
+            pltpu.SemaphoreType.DMA((halves,)),
+            pltpu.SemaphoreType.DMA((halves,)),
         ],
         compiler_params=params(63),
         name="feed_forward",

time: 134 us -> 134 us (level)
  no operation moved by 1% of the time
where the time goes in v4:
time: 134 us; the launch traced here: 133 us
  waiting for transfers between devices  53.4 us (40%)
  starting transfers between devices  39.6 us (30%)
  blocking collectives  16.9 us (13%)
  Pallas kernels  16.3 us (12%)
  local copies, waits for them, and re-layouts  4.42 us (3%)
  other arithmetic  2 us (1%)
    all_to_all x3, waiting for transfers between devices, exchange(): return lax.all_to_all(blocks, axes, split_axis=0, concat_axis=0, tiled=True)  51.8 us
    all_to_all x3, starting transfers between devices, exchange(): return lax.all_to_all(blocks, axes, split_axis=0, concat_axis=0, tiled=True)  32.8 us
    all_to_all x1, blocking collectives, exchange(): return lax.all_to_all(blocks, axes, split_axis=0, concat_axis=0, tiled=True)  16.9 us
    pallas_call x1, Pallas kernels, stack_weights(): pl.pallas_call(kernel, grid=(4,), in_specs=[columns(units)] * 6, out_spec...  7.13 us
    pallas_call x1, Pallas kernels, feed_forward(): pl.pallas_call(kernel, in_specs=[ANY] * 3, out_specs=ANY, out_shape=jax.S...  7.1 us
    ppermute x3, starting transfers between devices, local(): other = tuple((lax.ppermute(w, 'core', [(0, 1), (1, 0)]) for w in own))  6.77 us
  transfers between devices with their start and end apart: 6, of which 5 were waited for; matrix products, arithmetic and copies ran while one was open for 2% of the time, Pallas kernels for 5%

profile of v4, /device:TPU:1, one launch (start us, length us, event | category | flops | bytes accessed | tf_op | source)
XLA Modules:
  0.0 132.9 jit_solution(11643992472065880918)
XLA Ops:
  0.0 1.4 %broadcast_in_dim.32 = bf16[8,64,128]{2,1,0:T(8,128)(2,1)} broadcast(bf16[64,128]{1,0:T(8,128)(2,1)} %param.6), dimensions={1,2} | broadcast | bytes 147456 | tf_op jit(solution)/shard_map/broadcast_in_dim | solution.py:230
  1.4 15.6 %all-to-all-start = ((bf16[8,64,128]{2,1,0:T(8,128)(2,1)}), bf16[8,64,128]{2,1,0:T(8,128)(2,1)S(1)}, u32[]{:S(2)}, u32[]{:S(2)}) async-start(bf16[8,64,128]{2,1,0:T(8,128)(2,1)} %broadcast_in_dim.32), calls=%async_computation | async-start | bytes 262144 | tf_op jit(solution)/shard_map/all_to_all | solution.py:215
  17.0 0.8 copy.25
  17.8 0.1 eq.28
  17.9 0.1 fusion.2
  18.0 0.2 reduce_window_sum.11
  18.2 0.2 select_reduce_fusion.1
  18.3 0.1 reduce_sum.33
  18.6 0.7 multiply_add_fusion
  19.3 0.1 fusion.1
  19.4 0.1 copy.30
  19.5 10.7 %all-to-all-done.x_ref = bf16[8,64,128]{2,1,0:T(8,128)(2,1)S(1)} async-done(((bf16[8,64,128]{2,1,0:T(8,128)(2,1)}), bf16[8,64,128]{2,1,0:T(8,128)(2,1)S(1)}, u32[]{:S(2)}, u32[]{:S(2)}) %all-to-all-start) | async-done | bytes 131104 | tf_op jit(solution)/shard_map/all_to_all | solution.py:215
  30.2 1.6 %dispatch.1 = bf16[8,2,2,2,16,1024]{5,4,3,2,1,0:T(8,128)(2,1)} custom-call(bf16[256,64]{1,0:T(8,128)(2,1)S(1)} %bitcast.10, bf16[8,64,128]{2,1,0:T(8,128)(2,1)S(1)} %all-to-all-done.x_ref), custom_call_target="tpu_custom_call" | custom-call | tf_op jit(solution)/shard_map/dispatch/pallas_call | solution.py:43
  31.8 12.0 %all-to-all-start.1 = ((bf16[64,16,1024]{2,1,0:T(8,128)(2,1)}), bf16[64,16,1024]{2,1,0:T(8,128)(2,1)}, u32[]{:S(2)}, u32[]{:S(2)}) async-start(bf16[64,16,1024]{2,1,0:T(8,128)(2,1)} %bitcast.3), calls=%async_computation.1 | async-start | bytes 4194304 | tf_op jit(solution)/shard_map/all_to_all | solution.py:215
  43.8 2.4 %collective-permute-start = (bf16[172,4096]{1,0:T(8,128)(2,1)S(1)}, bf16[172,4096]{1,0:T(8,128)(2,1)S(1)}, u32[]{:S(2)}, u32[]{:S(2)}) collective-permute-start(bf16[172,4096]{1,0:T(8,128)(2,1)S(1)} %bitcast.14), channel_id=1, source_target_pairs={{0,1},{1,0},{2,3},{3,2},{4,5},{5,4},{6,7},{7,6},{8,9},{9,8},{10,11... | collective-permute-start | bytes 4227080 | tf_op jit(solution)/shard_map/ppermute | solution.py:244
  46.3 1.9 %collective-permute-start.1 = (bf16[172,4096]{1,0:T(8,128)(2,1)S(1)}, bf16[172,4096]{1,0:T(8,128)(2,1)S(1)}, u32[]{:S(2)}, u32[]{:S(2)}) collective-permute-start(bf16[172,4096]{1,0:T(8,128)(2,1)S(1)} %bitcast.16), channel_id=1, source_target_pairs={{0,1},{1,0},{2,3},{3,2},{4,5},{5,4},{6,7},{7,6},{8,9},{9,8},{10,11... | collective-permute-start | bytes 4227080 | tf_op jit(solution)/shard_map/ppermute | solution.py:244
  48.2 2.4 %collective-permute-start.2 = (bf16[172,4096]{1,0:T(8,128)(2,1)}, bf16[172,4096]{1,0:T(8,128)(2,1)}, u32[]{:S(2)}, u32[]{:S(2)}) collective-permute-start(bf16[172,4096]{1,0:T(8,128)(2,1)} %bitcast.17), channel_id=1, source_target_pairs={{0,1},{1,0},{2,3},{3,2},{4,5},{5,4},{6,7},{7,6},{8,9},{9,8},{10,11... | collective-permute-start | bytes 4227080 | tf_op jit(solution)/shard_map/ppermute | solution.py:244
  50.6 0.8 collective-permute-done.1.ou
  51.4 0.4 copy-done.2
  51.8 1.1 copy-done.3
  52.9 0.9 collective-permute-done.2.od
  53.8 7.1 %stack_weights.1 = (bf16[704,4096]{1,0:T(8,128)(2,1)}, bf16[352,4096]{1,0:T(8,128)(2,1)}) custom-call(bf16[172,4096]{1,0:T(8,128)(2,1)} %bitcast.13, bf16[172,4096]{1,0:T(8,128)(2,1)} %bitcast.15, bf16[172,4096]{1,0:T(8,128)(2,1)} %bitcast.18, bf16[172,4096]{1,0:T(8,128)(2,1)} %copy-done.2, bf16[172,4096]{1,0:T(8,128)(2,1)} %copy-done.3, ...), custom_call_target="tpu_custom_call" | custom-call | bytes 16908288 | tf_op jit(solution)/shard_map/stack_weights/pallas_call | solution.py:72
  60.9 12.2 %all-to-all-done.1.x_ref = bf16[64,16,1024]{2,1,0:T(8,128)(2,1)} async-done(((bf16[64,16,1024]{2,1,0:T(8,128)(2,1)}), bf16[64,16,1024]{2,1,0:T(8,128)(2,1)}, u32[]{:S(2)}, u32[]{:S(2)}) %all-to-all-start.1) | async-done | bytes 2097184 | tf_op jit(solution)/shard_map/all_to_all | solution.py:215
  73.1 7.1 %feed_forward.1 = bf16[16,4,16,1024]{3,2,1,0:T(8,128)(2,1)} custom-call(bf16[64,16,1024]{2,1,0:T(8,128)(2,1)} %all-to-all-done.1.x_ref, bf16[704,4096]{1,0:T(8,128)(2,1)} %get-tuple-element.7.f_ref, bf16[352,4096]{1,0:T(8,128)(2,1)} %get-tuple-element.8.l_ref), custom_call_target="tpu_custom_call" | custom-call | tf_op jit(solution)/shard_map/feed_forward/pallas_call | solution.py:158
  80.3 5.2 %all-to-all-start.2 = ((bf16[64,16,1024]{2,1,0:T(8,128)(2,1)}), bf16[64,16,1024]{2,1,0:T(8,128)(2,1)S(1)}, u32[]{:S(2)}, u32[]{:S(2)}) async-start(bf16[64,16,1024]{2,1,0:T(8,128)(2,1)} %bitcast.11), calls=%async_computation.2 | async-start | bytes 4194304 | tf_op jit(solution)/shard_map/all_to_all | solution.py:215
  85.5 0.1 select_reduce_fusion
  85.6 0.1 copy.27
  85.7 0.2 copy.28
  86.0 28.9 %all-to-all-done.2 = bf16[64,16,1024]{2,1,0:T(8,128)(2,1)S(1)} async-done(((bf16[64,16,1024]{2,1,0:T(8,128)(2,1)}), bf16[64,16,1024]{2,1,0:T(8,128)(2,1)S(1)}, u32[]{:S(2)}, u32[]{:S(2)}) %all-to-all-start.2) | async-done | bytes 2097184 | tf_op jit(solution)/shard_map/all_to_all | solution.py:215
  114.9 0.5 combine.1
  115.3 16.9 %all_to_all.20 = bf16[8,64,128]{2,1,0:T(8,128)(2,1)S(1)} all-to-all(bf16[8,64,128]{2,1,0:T(8,128)(2,1)S(1)} %combine.1), channel_id=1, replica_groups=mesh['expert'=16,'far'=8,'near'=2,'core'=2] {'far'}, dimensions={0} | all-to-all | bytes 262144 | tf_op jit(solution)/shard_map/all_to_all | solution.py:215
  132.2 0.6 reduce_sum.35
  (14 shorter events, 0.2 us)
Async XLA Ops:
  1.4 28.8 %all-to-all-start = ((bf16[8,64,128]{2,1,0:T(8,128)(2,1)}), bf16[8,64,128]{2,1,0:T(8,128)(2,1)S(1)}, u32[]{:S(2)}, u32[]{:S(2)}) async-start(bf16[8,64,128]{2,1,0:T(8,128)(2,1)} %broadcast_in_dim.32), calls=%async_computation | async-start | bytes 262144 | tf_op jit(solution)/shard_map/all_to_all | solution.py:215
  31.8 12.0 %copy-start = (bf16[1,172,4096]{2,1,0:T(8,128)(2,1)S(1)}, bf16[1,172,4096]{2,1,0:T(8,128)(2,1)}, u32[]{:S(2)}) copy-start(bf16[1,172,4096]{2,1,0:T(8,128)(2,1)} %param.9) | copy-start | bytes 4227076
  31.8 14.5 %copy-start.1 = (bf16[1,172,4096]{2,1,0:T(8,128)(2,1)S(1)}, bf16[1,172,4096]{2,1,0:T(8,128)(2,1)}, u32[]{:S(2)}) copy-start(bf16[1,172,4096]{2,1,0:T(8,128)(2,1)} %param.10) | copy-start | bytes 4227076
  31.8 41.3 %all-to-all-start.1 = ((bf16[64,16,1024]{2,1,0:T(8,128)(2,1)}), bf16[64,16,1024]{2,1,0:T(8,128)(2,1)}, u32[]{:S(2)}, u32[]{:S(2)}) async-start(bf16[64,16,1024]{2,1,0:T(8,128)(2,1)} %bitcast.3), calls=%async_computation.1 | async-start | bytes 4194304 | tf_op jit(solution)/shard_map/all_to_all | solution.py:215
  43.8 6.8 %collective-permute-start = (bf16[172,4096]{1,0:T(8,128)(2,1)S(1)}, bf16[172,4096]{1,0:T(8,128)(2,1)S(1)}, u32[]{:S(2)}, u32[]{:S(2)}) collective-permute-start(bf16[172,4096]{1,0:T(8,128)(2,1)S(1)} %bitcast.14), channel_id=1, source_target_pairs={{0,1},{1,0},{2,3},{3,2},{4,5},{5,4},{6,7},{7,6},{8,9},{9,8},{10,11... | collective-permute-start | bytes 4227080 | tf_op jit(solution)/shard_map/ppermute | solution.py:244
  46.3 5.1 %collective-permute-start.1 = (bf16[172,4096]{1,0:T(8,128)(2,1)S(1)}, bf16[172,4096]{1,0:T(8,128)(2,1)S(1)}, u32[]{:S(2)}, u32[]{:S(2)}) collective-permute-start(bf16[172,4096]{1,0:T(8,128)(2,1)S(1)} %bitcast.16), channel_id=1, source_target_pairs={{0,1},{1,0},{2,3},{3,2},{4,5},{5,4},{6,7},{7,6},{8,9},{9,8},{10,11... | collective-permute-start | bytes 4227080 | tf_op jit(solution)/shard_map/ppermute | solution.py:244
  48.2 5.6 %collective-permute-start.2 = (bf16[172,4096]{1,0:T(8,128)(2,1)}, bf16[172,4096]{1,0:T(8,128)(2,1)}, u32[]{:S(2)}, u32[]{:S(2)}) collective-permute-start(bf16[172,4096]{1,0:T(8,128)(2,1)} %bitcast.17), channel_id=1, source_target_pairs={{0,1},{1,0},{2,3},{3,2},{4,5},{5,4},{6,7},{7,6},{8,9},{9,8},{10,11... | collective-permute-start | bytes 4227080 | tf_op jit(solution)/shard_map/ppermute | solution.py:244
  50.6 1.1 copy-start.2
  51.8 1.1 copy-start.3
  80.2 5.2 %copy-start.4 = (f32[64,2]{0,1:T(2,128)S(1)}, f32[64,2]{0,1:T(2,128)}, u32[]{:S(2)}) copy-start(f32[64,2]{0,1:T(2,128)} %param.8) | copy-start | bytes 1540
  80.3 34.6 %all-to-all-start.2 = ((bf16[64,16,1024]{2,1,0:T(8,128)(2,1)}), bf16[64,16,1024]{2,1,0:T(8,128)(2,1)S(1)}, u32[]{:S(2)}, u32[]{:S(2)}) async-start(bf16[64,16,1024]{2,1,0:T(8,128)(2,1)} %bitcast.11), calls=%async_computation.2 | async-start | bytes 4194304 | tf_op jit(solution)/shard_map/all_to_all | solution.py:215

commit v5 on v4

--- a/solution.py
+++ b/solution.py
@@ -49,7 +49,7 @@
             pltpu.VMEM((steps, experts, cores, slots, per * lanes), BF),
             pltpu.SemaphoreType.DMA((steps, 4)),
         ],
-        compiler_params=params(8),
+        compiler_params=params(52),
         name="dispatch",
     )(select, gathered)
 
@@ -59,12 +59,10 @@
     tall = -(-units // 16) * 16
     span = features // 4
 
-    def kernel(g, u, d, og, ou, od, first_ref, last_ref):
+    def kernel(g, u, d, og, ou, od, out_ref):
         blank = jnp.zeros((tall - units, span), BF)
-        for i, src in enumerate((g, og, u, ou)):
-            first_ref[i * tall : (i + 1) * tall] = jnp.concatenate([src[...], blank], axis=0)
-        for i, src in enumerate((d, od)):
-            last_ref[i * tall : (i + 1) * tall] = jnp.concatenate([src[...], blank], axis=0)
+        for i, src in enumerate((g, og, u, ou, d, od)):
+            out_ref[i * tall : (i + 1) * tall] = jnp.concatenate([src[...], blank], axis=0)
 
     def columns(rows):
         return pl.BlockSpec((rows, span), lambda i: (0, i))
@@ -73,12 +71,9 @@
         kernel,
         grid=(4,),
         in_specs=[columns(units)] * 6,
-        out_specs=[columns(4 * tall), columns(2 * tall)],
-        out_shape=[
-            jax.ShapeDtypeStruct((4 * tall, features), BF),
-            jax.ShapeDtypeStruct((2 * tall, features), BF),
-        ],
-        compiler_params=params(63),
+        out_specs=columns(6 * tall),
+        out_shape=jax.ShapeDtypeStruct((6 * tall, features), BF),
+        compiler_params=params(56),
         name="stack_weights",
         cost_estimate=pl.CostEstimate(
             flops=0, bytes_accessed=24 * units * features, transcendentals=0
@@ -86,9 +81,9 @@
     )(*own, *other)
 
 
-def feed_forward(incoming, first, last):
+def feed_forward(incoming, stacks, after):
     blocks, slots, width = incoming.shape
-    tall, features = last.shape
+    tall, features = stacks.shape[0] // 3, stacks.shape[1]
     ways = features // width
     groups = blocks // ways
     rows = groups * slots
@@ -98,28 +93,22 @@
     parts = lanes // 128
     halves = 2
 
-    def kernel(x_ref, f_ref, l_ref, o_ref, xs, ws, ds, total, hidden, ys, sx, sw, sd, so):
+    def kernel(x_ref, w_ref, _, o_ref, ws, ds, total, hidden, sw, sd):
         loads = []
         for t in range(steps):
             at = pl.ds(t * span, span)
-            x_at = x_ref.at[:, :, pl.ds(t * lanes, lanes)]
-            loads.append(
-                [
-                    pltpu.make_async_copy(x_at, xs.at[t], sx.at[t]),
-                    pltpu.make_async_copy(f_ref.at[:, at], ws.at[t], sw.at[t]),
-                ]
-            )
+            first = w_ref.at[pl.ds(0, 2 * tall), at]
+            loads.append(pltpu.make_async_copy(first, ws.at[t], sw.at[t]))
         for t in range(halves):
             at = pl.ds(t * features // halves, features // halves)
-            loads.append([pltpu.make_async_copy(l_ref.at[:, at], ds.at[t], sd.at[t])])
+            last = w_ref.at[pl.ds(2 * tall, tall), at]
+            loads.append(pltpu.make_async_copy(last, ds.at[t], sd.at[t]))
         for load in loads:
-            for copy in load:
-                copy.start()
+            load.start()
 
         for t in range(steps):
-            for copy in loads[t]:
-                copy.wait()
-            x = xs[t].reshape(groups, ways, slots, lanes)
+            loads[t].wait()
+            x = x_ref[:, :, t * lanes : (t + 1) * lanes].reshape(groups, ways, slots, lanes)
             x = jnp.concatenate(
                 [
                     x[:, k, :, p * 128 : (p + 1) * 128].reshape(rows, 128)
@@ -138,43 +127,31 @@
         gate, up = total[:, :tall], total[:, tall:]
         hidden[...] = (gate / (1.0 + jnp.exp(-gate)) * up).astype(BF)
 
-        stores = []
         for t in range(halves):
-            for copy in loads[steps + t]:
-                copy.wait()
+            loads[steps + t].wait()
             y = jnp.dot(hidden[...], ds[t], preferred_element_type=F32).astype(BF)
             for p in range(width // halves // 128):
                 for k in range(ways):
                     at = (p * ways + k) * 128
-                    ys[t, :, k, :, p * 128 : (p + 1) * 128] = y[:, at : at + 128].reshape(
-                        groups, slots, 128
-                    )
-            out = o_ref.at[:, :, :, pl.ds(t * width // halves, width // halves)]
-            stores.append(pltpu.make_async_copy(ys.at[t], out, so.at[t]))
-            stores[-1].start()
-        for copy in stores:
-            copy.wait()
+                    to = t * width // halves + p * 128
+                    o_ref[:, k, :, to : to + 128] = y[:, at : at + 128].reshape(groups, slots, 128)
 
     out = pl.pallas_call(
         kernel,
-        in_specs=[ANY] * 3,
-        out_specs=ANY,
+        in_specs=[VMEM, ANY, ANY],
+        out_specs=VMEM,
         out_shape=jax.ShapeDtypeStruct((groups, ways, slots, width), BF),
         scratch_shapes=[
-            pltpu.VMEM((steps, blocks, slots, lanes), BF),
             pltpu.VMEM((steps, 2 * tall, span), BF),
             pltpu.VMEM((halves, tall, features // halves), BF),
             pltpu.VMEM((rows, 2 * tall), F32),
             pltpu.VMEM((rows, tall), BF),
-            pltpu.VMEM((halves, groups, ways, slots, width // halves), BF),
-            pltpu.SemaphoreType.DMA((steps,)),
             pltpu.SemaphoreType.DMA((steps,)),
             pltpu.SemaphoreType.DMA((halves,)),
-            pltpu.SemaphoreType.DMA((halves,)),
         ],
-        compiler_params=params(63),
+        compiler_params=params(46),
         name="feed_forward",
-    )(incoming, first, last)
+    )(incoming, stacks, after)
     return out.reshape(blocks, slots, width)
 
 
@@ -243,9 +220,9 @@
     own = (gate_weight[0], up_weight[0], down_weight[0])
     other = tuple(lax.ppermute(w, "core", [(0, 1), (1, 0)]) for w in own)
     incoming = exchange(outgoing.reshape(blocks, slots, width), WIDE)
-    first, last = stack_weights(own, other)
-
-    result = feed_forward(incoming, first, last)
+    stacks = stack_weights(own, other)
+
+    result = feed_forward(incoming, stacks, mix)
 
     returned = exchange(result, WIDE)
     mixed = combine(mix, returned.reshape(blocks * slots, width), planes)

time: 134 us -> 132 us (0.985)
  blocking collectives: 16.9 us -> 51.3 us
  waiting for transfers between devices: 53.4 us -> 25.7 us
  starting transfers between devices: 39.6 us -> 33.9 us
  local copies, waits for them, and re-layouts: 4.42 us -> 2.93 us
    all_to_all x1 -> x2, blocking collectives: 16.9 us -> 51.3 us  [exchange(): return lax.all_to_all(blocks, axes, split_axis=0, concat_axis=0, tiled=True)]
    all_to_all x3 -> x2, waiting for transfers between devices: 51.8 us -> 23.1 us  [exchange(): return lax.all_to_all(blocks, axes, split_axis=0, concat_axis=0, tiled=True)]
    all_to_all x3 -> x2, starting transfers between devices: 32.8 us -> 27.2 us  [exchange(): return lax.all_to_all(blocks, axes, split_axis=0, concat_axis=0, tiled=True)]
    unnamed x11 -> x3, local copies, waits for them, and re-layouts: 2.26 us -> 0.77 us
  transfers between devices with their start and end apart: 6 -> 5, of which waited for: 5 -> 4; matrix products, arithmetic and copies ran while one was open for 2% -> 2% of each run, Pallas kernels for 5% -> 5%
where the time goes in v5:
time: 132 us; the launch traced here: 131 us
  blocking collectives  51.3 us (39%)
  starting transfers between devices  33.9 us (26%)
  waiting for transfers between devices  25.7 us (19%)
  Pallas kernels  15.2 us (12%)
  local copies, waits for them, and re-layouts  2.93 us (2%)
  other arithmetic  2 us (2%)
    all_to_all x2, blocking collectives, exchange(): return lax.all_to_all(blocks, axes, split_axis=0, concat_axis=0, tiled=True)  51.3 us
    all_to_all x2, starting transfers between devices, exchange(): return lax.all_to_all(blocks, axes, split_axis=0, concat_axis=0, tiled=True)  27.2 us
    all_to_all x2, waiting for transfers between devices, exchange(): return lax.all_to_all(blocks, axes, split_axis=0, concat_axis=0, tiled=True)  23.1 us
    pallas_call x1, Pallas kernels, stack_weights(): pl.pallas_call(kernel, grid=(4,), in_specs=[columns(units)] * 6, out_spec...  7.12 us
    ppermute x3, starting transfers between devices, local(): other = tuple((lax.ppermute(w, 'core', [(0, 1), (1, 0)]) for w in own))  6.7 us
    pallas_call x1, Pallas kernels, feed_forward(): pl.pallas_call(kernel, in_specs=[VMEM, ANY, ANY], out_specs=VMEM, out_sha...  6 us
  transfers between devices with their start and end apart: 5, of which 4 were waited for; matrix products, arithmetic and copies ran while one was open for 2% of the time, Pallas kernels for 5%

profile of v5, /device:TPU:1, one launch (start us, length us, event | category | flops | bytes accessed | tf_op | source)
XLA Modules:
  0.0 131.2 jit_solution(10779718235719209536)
XLA Ops:
  0.0 1.4 %broadcast_in_dim.32 = bf16[8,64,128]{2,1,0:T(8,128)(2,1)} broadcast(bf16[64,128]{1,0:T(8,128)(2,1)} %param.6), dimensions={1,2} | broadcast | bytes 147456 | tf_op jit(solution)/shard_map/broadcast_in_dim | solution.py:207
  1.4 15.6 %all-to-all-start = ((bf16[8,64,128]{2,1,0:T(8,128)(2,1)}), bf16[8,64,128]{2,1,0:T(8,128)(2,1)S(1)}, u32[]{:S(2)}, u32[]{:S(2)}) async-start(bf16[8,64,128]{2,1,0:T(8,128)(2,1)} %broadcast_in_dim.32), calls=%async_computation | async-start | bytes 262144 | tf_op jit(solution)/shard_map/all_to_all | solution.py:192
  17.0 0.8 copy.25
  17.8 0.1 eq.28
  17.9 0.1 fusion.2
  18.0 0.2 reduce_window_sum.11
  18.2 0.2 select_reduce_fusion.1
  18.4 0.1 reduce_sum.33
  18.5 0.1 copy.26
  18.6 0.7 multiply_add_fusion
  19.3 0.1 fusion.1
  19.4 0.1 copy.30
  19.5 10.7 %all-to-all-done.x_ref = bf16[8,64,128]{2,1,0:T(8,128)(2,1)S(1)} async-done(((bf16[8,64,128]{2,1,0:T(8,128)(2,1)}), bf16[8,64,128]{2,1,0:T(8,128)(2,1)S(1)}, u32[]{:S(2)}, u32[]{:S(2)}) %all-to-all-start) | async-done | bytes 131104 | tf_op jit(solution)/shard_map/all_to_all | solution.py:192
  30.2 1.7 %dispatch.1 = bf16[8,2,2,2,16,1024]{5,4,3,2,1,0:T(8,128)(2,1)} custom-call(bf16[256,64]{1,0:T(8,128)(2,1)S(1)} %bitcast.11, bf16[8,64,128]{2,1,0:T(8,128)(2,1)S(1)} %all-to-all-done.x_ref), custom_call_target="tpu_custom_call" | custom-call | tf_op jit(solution)/shard_map/dispatch/pallas_call | solution.py:43
  31.8 0.0 copy-start
  31.9 11.5 %all-to-all-start.1 = ((bf16[64,16,1024]{2,1,0:T(8,128)(2,1)}), bf16[64,16,1024]{2,1,0:T(8,128)(2,1)S(1)}, u32[]{:S(2)}, u32[]{:S(2)}) async-start(bf16[64,16,1024]{2,1,0:T(8,128)(2,1)} %bitcast.12), calls=%async_computation.1 | async-start | bytes 4194304 | tf_op jit(solution)/shard_map/all_to_all | solution.py:192
  43.4 2.4 %collective-permute-start = (bf16[172,4096]{1,0:T(8,128)(2,1)}, bf16[172,4096]{1,0:T(8,128)(2,1)}, u32[]{:S(2)}, u32[]{:S(2)}) collective-permute-start(bf16[172,4096]{1,0:T(8,128)(2,1)} %bitcast.4.g), channel_id=1, source_target_pairs={{0,1},{1,0},{2,3},{3,2},{4,5},{5,4},{6,7},{7,6},{8,9},{9,8},{10,11... | collective-permute-start | bytes 4227080 | tf_op jit(solution)/shard_map/ppermute | solution.py:221
  45.8 2.0 %collective-permute-start.1 = (bf16[172,4096]{1,0:T(8,128)(2,1)}, bf16[172,4096]{1,0:T(8,128)(2,1)}, u32[]{:S(2)}, u32[]{:S(2)}) collective-permute-start(bf16[172,4096]{1,0:T(8,128)(2,1)} %bitcast.5.u), channel_id=1, source_target_pairs={{0,1},{1,0},{2,3},{3,2},{4,5},{5,4},{6,7},{7,6},{8,9},{9,8},{10,11... | collective-permute-start | bytes 4227080 | tf_op jit(solution)/shard_map/ppermute | solution.py:221
  47.8 2.4 %collective-permute-start.2 = (bf16[172,4096]{1,0:T(8,128)(2,1)}, bf16[172,4096]{1,0:T(8,128)(2,1)}, u32[]{:S(2)}, u32[]{:S(2)}) collective-permute-start(bf16[172,4096]{1,0:T(8,128)(2,1)} %bitcast.6.d), channel_id=1, source_target_pairs={{0,1},{1,0},{2,3},{3,2},{4,5},{5,4},{6,7},{7,6},{8,9},{9,8},{10,11... | collective-permute-start | bytes 4227080 | tf_op jit(solution)/shard_map/ppermute | solution.py:221
  50.1 0.1 select_reduce_fusion
  50.2 0.1 copy.27
  50.3 0.1 broadcast_in_dim.31
  50.4 0.2 copy.28
  50.7 0.6 collective-permute-done.1.ou
  51.2 2.1 %collective-permute-done.2.od = bf16[172,4096]{1,0:T(8,128)(2,1)} collective-permute-done((bf16[172,4096]{1,0:T(8,128)(2,1)}, bf16[172,4096]{1,0:T(8,128)(2,1)}, u32[]{:S(2)}, u32[]{:S(2)}) %collective-permute-start.2) | collective-permute-done | bytes 1409056 | tf_op jit(solution)/shard_map/ppermute | solution.py:221
  53.3 7.1 %stack_weights.1.w_ref = bf16[1056,4096]{1,0:T(8,128)(2,1)} custom-call(bf16[172,4096]{1,0:T(8,128)(2,1)} %bitcast.4.g, bf16[172,4096]{1,0:T(8,128)(2,1)} %bitcast.5.u, bf16[172,4096]{1,0:T(8,128)(2,1)} %bitcast.6.d, bf16[172,4096]{1,0:T(8,128)(2,1)} %collective-permute-done.og, bf16[172,4096]{1,0:T(8,128)(2,1)} %collective-permute-done.1.ou, ...), custom_call_target="tpu_custom_call" | custom-call | bytes 16908288 | tf_op jit(solution)/shard_map/stack_weights/pallas_call | solution.py:70
  60.4 12.4 %all-to-all-done.1.x_ref = bf16[64,16,1024]{2,1,0:T(8,128)(2,1)S(1)} async-done(((bf16[64,16,1024]{2,1,0:T(8,128)(2,1)}), bf16[64,16,1024]{2,1,0:T(8,128)(2,1)S(1)}, u32[]{:S(2)}, u32[]{:S(2)}) %all-to-all-start.1) | async-done | bytes 2097184 | tf_op jit(solution)/shard_map/all_to_all | solution.py:192
  72.8 6.0 %feed_forward.1 = bf16[16,4,16,1024]{3,2,1,0:T(8,128)(2,1)S(1)} custom-call(bf16[64,16,1024]{2,1,0:T(8,128)(2,1)S(1)} %all-to-all-done.1.x_ref, bf16[1056,4096]{1,0:T(8,128)(2,1)} %stack_weights.1.w_ref, bf16[128,1024]{1,0:T(8,128)(2,1)S(1)} %pad_maximum_fusion._.w_ref), custom_call_target="tpu_custom_call" | custom-call | tf_op jit(solution)/shard_map/feed_forward/pallas_call | solution.py:139
  78.8 34.4 %all_to_all.20 = bf16[64,16,1024]{2,1,0:T(8,128)(2,1)S(1)} all-to-all(bf16[64,16,1024]{2,1,0:T(8,128)(2,1)S(1)} %bitcast.9), channel_id=1, replica_groups=mesh['expert'=16,'far'=8,'near'=2,'core'=2] {'expert','near','core'}, dimensions={0} | all-to-all | bytes 4194304 | tf_op jit(solution)/shard_map/all_to_all | solution.py:192
  113.2 0.5 combine.1
  113.7 16.9 %all_to_all.21 = bf16[8,64,128]{2,1,0:T(8,128)(2,1)S(1)} all-to-all(bf16[8,64,128]{2,1,0:T(8,128)(2,1)S(1)} %combine.1), channel_id=1, replica_groups=mesh['expert'=16,'far'=8,'near'=2,'core'=2] {'far'}, dimensions={0} | all-to-all | bytes 262144 | tf_op jit(solution)/shard_map/all_to_all | solution.py:192
  130.6 0.6 reduce_sum.35
  (5 shorter events, 0.1 us)
Async XLA Ops:
  1.4 28.8 %all-to-all-start = ((bf16[8,64,128]{2,1,0:T(8,128)(2,1)}), bf16[8,64,128]{2,1,0:T(8,128)(2,1)S(1)}, u32[]{:S(2)}, u32[]{:S(2)}) async-start(bf16[8,64,128]{2,1,0:T(8,128)(2,1)} %broadcast_in_dim.32), calls=%async_computation | async-start | bytes 262144 | tf_op jit(solution)/shard_map/all_to_all | solution.py:192
  31.8 18.3 %copy-start = (f32[64,2]{0,1:T(2,128)S(1)}, f32[64,2]{0,1:T(2,128)}, u32[]{:S(2)}) copy-start(f32[64,2]{0,1:T(2,128)} %param.8) | copy-start | bytes 1540
  31.9 41.0 %all-to-all-start.1 = ((bf16[64,16,1024]{2,1,0:T(8,128)(2,1)}), bf16[64,16,1024]{2,1,0:T(8,128)(2,1)S(1)}, u32[]{:S(2)}, u32[]{:S(2)}) async-start(bf16[64,16,1024]{2,1,0:T(8,128)(2,1)} %bitcast.12), calls=%async_computation.1 | async-start | bytes 4194304 | tf_op jit(solution)/shard_map/all_to_all | solution.py:192
  43.4 7.3 %collective-permute-start = (bf16[172,4096]{1,0:T(8,128)(2,1)}, bf16[172,4096]{1,0:T(8,128)(2,1)}, u32[]{:S(2)}, u32[]{:S(2)}) collective-permute-start(bf16[172,4096]{1,0:T(8,128)(2,1)} %bitcast.4.g), channel_id=1, source_target_pairs={{0,1},{1,0},{2,3},{3,2},{4,5},{5,4},{6,7},{7,6},{8,9},{9,8},{10,11... | collective-permute-start | bytes 4227080 | tf_op jit(solution)/shard_map/ppermute | solution.py:221
  45.8 5.5 %collective-permute-start.1 = (bf16[172,4096]{1,0:T(8,128)(2,1)}, bf16[172,4096]{1,0:T(8,128)(2,1)}, u32[]{:S(2)}, u32[]{:S(2)}) collective-permute-start(bf16[172,4096]{1,0:T(8,128)(2,1)} %bitcast.5.u), channel_id=1, source_target_pairs={{0,1},{1,0},{2,3},{3,2},{4,5},{5,4},{6,7},{7,6},{8,9},{9,8},{10,11... | collective-permute-start | bytes 4227080 | tf_op jit(solution)/shard_map/ppermute | solution.py:221
  47.8 5.5 %collective-permute-start.2 = (bf16[172,4096]{1,0:T(8,128)(2,1)}, bf16[172,4096]{1,0:T(8,128)(2,1)}, u32[]{:S(2)}, u32[]{:S(2)}) collective-permute-start(bf16[172,4096]{1,0:T(8,128)(2,1)} %bitcast.6.d), channel_id=1, source_target_pairs={{0,1},{1,0},{2,3},{3,2},{4,5},{5,4},{6,7},{7,6},{8,9},{9,8},{10,11... | collective-permute-start | bytes 4227080 | tf_op jit(solution)/shard_map/ppermute | solution.py:221

commit v6 on v5

--- a/solution.py
+++ b/solution.py
@@ -11,6 +11,7 @@
 TENSOR = ("far", "near", "core")
 WIDE = ("expert", "near", "core")
 ANY = pl.BlockSpec(memory_space=pl.ANY)
+NT = (((1,), (1,)), ((), ()))
 VMEM = pl.BlockSpec(memory_space=pltpu.VMEM)
 
 
@@ -88,17 +89,15 @@
     groups = blocks // ways
     rows = groups * slots
     steps = 4
-    lanes = width // steps
-    span = lanes * ways
-    parts = lanes // 128
+    cuts = [width * n // 8 for n in (0, 2, 4, 7, 8)]
     halves = 2
 
     def kernel(x_ref, w_ref, _, o_ref, ws, ds, total, hidden, sw, sd):
         loads = []
         for t in range(steps):
-            at = pl.ds(t * span, span)
+            at = pl.ds(cuts[t] * ways, (cuts[t + 1] - cuts[t]) * ways)
             first = w_ref.at[pl.ds(0, 2 * tall), at]
-            loads.append(pltpu.make_async_copy(first, ws.at[t], sw.at[t]))
+            loads.append(pltpu.make_async_copy(first, ws.at[:, at], sw.at[t]))
         for t in range(halves):
             at = pl.ds(t * features // halves, features // halves)
             last = w_ref.at[pl.ds(2 * tall, tall), at]
@@ -108,17 +107,18 @@
 
         for t in range(steps):
             loads[t].wait()
-            x = x_ref[:, :, t * lanes : (t + 1) * lanes].reshape(groups, ways, slots, lanes)
+            lanes = cuts[t + 1] - cuts[t]
+            x = x_ref[:, :, cuts[t] : cuts[t + 1]].reshape(groups, ways, slots, lanes)
             x = jnp.concatenate(
                 [
                     x[:, k, :, p * 128 : (p + 1) * 128].reshape(rows, 128)
-                    for p in range(parts)
+                    for p in range(lanes // 128)
                     for k in range(ways)
                 ],
                 axis=1,
             )
             part = lax.dot_general(
-                x, ws[t], (((1,), (1,)), ((), ())), preferred_element_type=F32
+                x, ws[:, cuts[t] * ways : cuts[t + 1] * ways], NT, preferred_element_type=F32
             )
             if t == 0:
                 total[...] = part
@@ -142,7 +142,7 @@
         out_specs=VMEM,
         out_shape=jax.ShapeDtypeStruct((groups, ways, slots, width), BF),
         scratch_shapes=[
-            pltpu.VMEM((steps, 2 * tall, span), BF),
+            pltpu.VMEM((2 * tall, features), BF),
             pltpu.VMEM((halves, tall, features // halves), BF),
             pltpu.VMEM((rows, 2 * tall), F32),
             pltpu.VMEM((rows, tall), BF),

time: 132 us -> 132 us (level)
  no operation moved by 1% of the time
where the time goes in v6:
time: 132 us; the launch traced here: 131 us
  blocking collectives  51.3 us (39%)
  starting transfers between devices  33.9 us (26%)
  waiting for transfers between devices  25.7 us (19%)
  Pallas kernels  15.4 us (12%)
  local copies, waits for them, and re-layouts  2.93 us (2%)
  other arithmetic  2 us (2%)
    all_to_all x2, blocking collectives, exchange(): return lax.all_to_all(blocks, axes, split_axis=0, concat_axis=0, tiled=True)  51.3 us
    all_to_all x2, starting transfers between devices, exchange(): return lax.all_to_all(blocks, axes, split_axis=0, concat_axis=0, tiled=True)  27.2 us
    all_to_all x2, waiting for transfers between devices, exchange(): return lax.all_to_all(blocks, axes, split_axis=0, concat_axis=0, tiled=True)  23.1 us
    pallas_call x1, Pallas kernels, stack_weights(): pl.pallas_call(kernel, grid=(4,), in_specs=[columns(units)] * 6, out_spec...  7.12 us
    ppermute x3, starting transfers between devices, local(): other = tuple((lax.ppermute(w, 'core', [(0, 1), (1, 0)]) for w in own))  6.7 us
    pallas_call x1, Pallas kernels, feed_forward(): pl.pallas_call(kernel, in_specs=[VMEM, ANY, ANY], out_specs=VMEM, out_sha...  6.12 us
  transfers between devices with their start and end apart: 5, of which 4 were waited for; matrix products, arithmetic and copies ran while one was open for 2% of the time, Pallas kernels for 5%

profile of v6, /device:TPU:1, one launch (start us, length us, event | category | flops | bytes accessed | tf_op | source)
XLA Modules:
  0.0 131.3 jit_solution(16498995150592579997)
XLA Ops:
  0.0 1.4 %broadcast_in_dim.32 = bf16[8,64,128]{2,1,0:T(8,128)(2,1)} broadcast(bf16[64,128]{1,0:T(8,128)(2,1)} %param.6), dimensions={1,2} | broadcast | bytes 147456 | tf_op jit(solution)/shard_map/broadcast_in_dim | solution.py:207
  1.4 15.6 %all-to-all-start = ((bf16[8,64,128]{2,1,0:T(8,128)(2,1)}), bf16[8,64,128]{2,1,0:T(8,128)(2,1)S(1)}, u32[]{:S(2)}, u32[]{:S(2)}) async-start(bf16[8,64,128]{2,1,0:T(8,128)(2,1)} %broadcast_in_dim.32), calls=%async_computation | async-start | bytes 262144 | tf_op jit(solution)/shard_map/all_to_all | solution.py:192
  17.0 0.8 copy.25
  17.8 0.1 eq.28
  17.9 0.1 fusion.2
  18.0 0.2 reduce_window_sum.11
  18.2 0.2 select_reduce_fusion.1
  18.4 0.1 reduce_sum.33
  18.5 0.1 copy.26
  18.6 0.7 multiply_add_fusion
  19.3 0.1 fusion.1
  19.4 0.1 copy.30
  19.5 10.7 %all-to-all-done.x_ref = bf16[8,64,128]{2,1,0:T(8,128)(2,1)S(1)} async-done(((bf16[8,64,128]{2,1,0:T(8,128)(2,1)}), bf16[8,64,128]{2,1,0:T(8,128)(2,1)S(1)}, u32[]{:S(2)}, u32[]{:S(2)}) %all-to-all-start) | async-done | bytes 131104 | tf_op jit(solution)/shard_map/all_to_all | solution.py:192
  30.2 1.7 %dispatch.1 = bf16[8,2,2,2,16,1024]{5,4,3,2,1,0:T(8,128)(2,1)} custom-call(bf16[256,64]{1,0:T(8,128)(2,1)S(1)} %bitcast.11, bf16[8,64,128]{2,1,0:T(8,128)(2,1)S(1)} %all-to-all-done.x_ref), custom_call_target="tpu_custom_call" | custom-call | tf_op jit(solution)/shard_map/dispatch/pallas_call | solution.py:44
  31.8 0.0 copy-start
  31.9 11.5 %all-to-all-start.1 = ((bf16[64,16,1024]{2,1,0:T(8,128)(2,1)}), bf16[64,16,1024]{2,1,0:T(8,128)(2,1)S(1)}, u32[]{:S(2)}, u32[]{:S(2)}) async-start(bf16[64,16,1024]{2,1,0:T(8,128)(2,1)} %bitcast.12), calls=%async_computation.1 | async-start | bytes 4194304 | tf_op jit(solution)/shard_map/all_to_all | solution.py:192
  43.4 2.4 %collective-permute-start = (bf16[172,4096]{1,0:T(8,128)(2,1)}, bf16[172,4096]{1,0:T(8,128)(2,1)}, u32[]{:S(2)}, u32[]{:S(2)}) collective-permute-start(bf16[172,4096]{1,0:T(8,128)(2,1)} %bitcast.4.g), channel_id=1, source_target_pairs={{0,1},{1,0},{2,3},{3,2},{4,5},{5,4},{6,7},{7,6},{8,9},{9,8},{10,11... | collective-permute-start | bytes 4227080 | tf_op jit(solution)/shard_map/ppermute | solution.py:221
  45.8 2.0 %collective-permute-start.1 = (bf16[172,4096]{1,0:T(8,128)(2,1)}, bf16[172,4096]{1,0:T(8,128)(2,1)}, u32[]{:S(2)}, u32[]{:S(2)}) collective-permute-start(bf16[172,4096]{1,0:T(8,128)(2,1)} %bitcast.5.u), channel_id=1, source_target_pairs={{0,1},{1,0},{2,3},{3,2},{4,5},{5,4},{6,7},{7,6},{8,9},{9,8},{10,11... | collective-permute-start | bytes 4227080 | tf_op jit(solution)/shard_map/ppermute | solution.py:221
  47.8 2.4 %collective-permute-start.2 = (bf16[172,4096]{1,0:T(8,128)(2,1)}, bf16[172,4096]{1,0:T(8,128)(2,1)}, u32[]{:S(2)}, u32[]{:S(2)}) collective-permute-start(bf16[172,4096]{1,0:T(8,128)(2,1)} %bitcast.6.d), channel_id=1, source_target_pairs={{0,1},{1,0},{2,3},{3,2},{4,5},{5,4},{6,7},{7,6},{8,9},{9,8},{10,11... | collective-permute-start | bytes 4227080 | tf_op jit(solution)/shard_map/ppermute | solution.py:221
  50.1 0.1 select_reduce_fusion
  50.2 0.1 copy.27
  50.3 0.1 broadcast_in_dim.31
  50.4 0.2 copy.28
  50.7 0.6 collective-permute-done.1.ou
  51.2 2.1 %collective-permute-done.2.od = bf16[172,4096]{1,0:T(8,128)(2,1)} collective-permute-done((bf16[172,4096]{1,0:T(8,128)(2,1)}, bf16[172,4096]{1,0:T(8,128)(2,1)}, u32[]{:S(2)}, u32[]{:S(2)}) %collective-permute-start.2) | collective-permute-done | bytes 1409056 | tf_op jit(solution)/shard_map/ppermute | solution.py:221
  53.3 7.1 %stack_weights.1.w_ref = bf16[1056,4096]{1,0:T(8,128)(2,1)} custom-call(bf16[172,4096]{1,0:T(8,128)(2,1)} %bitcast.4.g, bf16[172,4096]{1,0:T(8,128)(2,1)} %bitcast.5.u, bf16[172,4096]{1,0:T(8,128)(2,1)} %bitcast.6.d, bf16[172,4096]{1,0:T(8,128)(2,1)} %collective-permute-done.og, bf16[172,4096]{1,0:T(8,128)(2,1)} %collective-permute-done.1.ou, ...), custom_call_target="tpu_custom_call" | custom-call | bytes 16908288 | tf_op jit(solution)/shard_map/stack_weights/pallas_call | solution.py:71
  60.4 12.4 %all-to-all-done.1.x_ref = bf16[64,16,1024]{2,1,0:T(8,128)(2,1)S(1)} async-done(((bf16[64,16,1024]{2,1,0:T(8,128)(2,1)}), bf16[64,16,1024]{2,1,0:T(8,128)(2,1)S(1)}, u32[]{:S(2)}, u32[]{:S(2)}) %all-to-all-start.1) | async-done | bytes 2097184 | tf_op jit(solution)/shard_map/all_to_all | solution.py:192
  72.8 6.1 %feed_forward.1 = bf16[16,4,16,1024]{3,2,1,0:T(8,128)(2,1)S(1)} custom-call(bf16[64,16,1024]{2,1,0:T(8,128)(2,1)S(1)} %all-to-all-done.1.x_ref, bf16[1056,4096]{1,0:T(8,128)(2,1)} %stack_weights.1.w_ref, bf16[128,1024]{1,0:T(8,128)(2,1)S(1)} %pad_maximum_fusion._.w_ref), custom_call_target="tpu_custom_call" | custom-call | tf_op jit(solution)/shard_map/feed_forward/pallas_call | solution.py:139
  78.9 34.4 %all_to_all.20 = bf16[64,16,1024]{2,1,0:T(8,128)(2,1)S(1)} all-to-all(bf16[64,16,1024]{2,1,0:T(8,128)(2,1)S(1)} %bitcast.9), channel_id=1, replica_groups=mesh['expert'=16,'far'=8,'near'=2,'core'=2] {'expert','near','core'}, dimensions={0} | all-to-all | bytes 4194304 | tf_op jit(solution)/shard_map/all_to_all | solution.py:192
  113.3 0.5 combine.1
  113.8 16.9 %all_to_all.21 = bf16[8,64,128]{2,1,0:T(8,128)(2,1)S(1)} all-to-all(bf16[8,64,128]{2,1,0:T(8,128)(2,1)S(1)} %combine.1), channel_id=1, replica_groups=mesh['expert'=16,'far'=8,'near'=2,'core'=2] {'far'}, dimensions={0} | all-to-all | bytes 262144 | tf_op jit(solution)/shard_map/all_to_all | solution.py:192
  130.7 0.6 reduce_sum.35
  (5 shorter events, 0.1 us)
Async XLA Ops:
  1.4 28.8 %all-to-all-start = ((bf16[8,64,128]{2,1,0:T(8,128)(2,1)}), bf16[8,64,128]{2,1,0:T(8,128)(2,1)S(1)}, u32[]{:S(2)}, u32[]{:S(2)}) async-start(bf16[8,64,128]{2,1,0:T(8,128)(2,1)} %broadcast_in_dim.32), calls=%async_computation | async-start | bytes 262144 | tf_op jit(solution)/shard_map/all_to_all | solution.py:192
  31.8 18.3 %copy-start = (f32[64,2]{0,1:T(2,128)S(1)}, f32[64,2]{0,1:T(2,128)}, u32[]{:S(2)}) copy-start(f32[64,2]{0,1:T(2,128)} %param.8) | copy-start | bytes 1540
  31.9 41.0 %all-to-all-start.1 = ((bf16[64,16,1024]{2,1,0:T(8,128)(2,1)}), bf16[64,16,1024]{2,1,0:T(8,128)(2,1)S(1)}, u32[]{:S(2)}, u32[]{:S(2)}) async-start(bf16[64,16,1024]{2,1,0:T(8,128)(2,1)} %bitcast.12), calls=%async_computation.1 | async-start | bytes 4194304 | tf_op jit(solution)/shard_map/all_to_all | solution.py:192
  43.4 7.3 %collective-permute-start = (bf16[172,4096]{1,0:T(8,128)(2,1)}, bf16[172,4096]{1,0:T(8,128)(2,1)}, u32[]{:S(2)}, u32[]{:S(2)}) collective-permute-start(bf16[172,4096]{1,0:T(8,128)(2,1)} %bitcast.4.g), channel_id=1, source_target_pairs={{0,1},{1,0},{2,3},{3,2},{4,5},{5,4},{6,7},{7,6},{8,9},{9,8},{10,11... | collective-permute-start | bytes 4227080 | tf_op jit(solution)/shard_map/ppermute | solution.py:221
  45.8 5.5 %collective-permute-start.1 = (bf16[172,4096]{1,0:T(8,128)(2,1)}, bf16[172,4096]{1,0:T(8,128)(2,1)}, u32[]{:S(2)}, u32[]{:S(2)}) collective-permute-start(bf16[172,4096]{1,0:T(8,128)(2,1)} %bitcast.5.u), channel_id=1, source_target_pairs={{0,1},{1,0},{2,3},{3,2},{4,5},{5,4},{6,7},{7,6},{8,9},{9,8},{10,11... | collective-permute-start | bytes 4227080 | tf_op jit(solution)/shard_map/ppermute | solution.py:221
  47.8 5.5 %collective-permute-start.2 = (bf16[172,4096]{1,0:T(8,128)(2,1)}, bf16[172,4096]{1,0:T(8,128)(2,1)}, u32[]{:S(2)}, u32[]{:S(2)}) collective-permute-start(bf16[172,4096]{1,0:T(8,128)(2,1)} %bitcast.6.d), channel_id=1, source_target_pairs={{0,1},{1,0},{2,3},{3,2},{4,5},{5,4},{6,7},{7,6},{8,9},{9,8},{10,11... | collective-permute-start | bytes 4227080 | tf_op jit(solution)/shard_map/ppermute | solution.py:221
